TPU v7x, 256 devices: a whole 4x4x8 slice. The times are simulated.
256 devices in a mesh: energy: 128 (over y_hi, z, x, core), mom: 2 (over y_lo).
Axes of the slice: x: 4, y: 4 (y_hi: 2, y_lo: 2; y = y_hi * 2 + y_lo), z: 8, core: 2. Of those that a mesh axis runs over, the one named last changes fastest.
Arguments:
- hamiltonian: float32 [2, 2, 2, 128, 128], P('mom'), may hold values from -0.125 to 0.125
- hopping: float32 [2, 2, 128, 128], P('mom'), may hold values from -0.21875 to 0.21875
- self_energy: float32 [2, 128, 2, 2, 128, 128], P('mom', 'energy'), may hold values from -0.078125 to 0.078125
- screened: float32 [2, 128, 2, 2, 128, 128], P('mom', 'energy'), may hold values from -24 to 24
- energy_map: int32 [128], P('energy'), may hold values from 0 to 127, each once
Outputs:
- new_sigma: float32 [2, 128, 2, 2, 128, 128], P('mom', 'energy')
- polar: float32 [2, 2, 128, 32768], P('mom', None, None, 'energy')
Inputs may be any that keep to these rules, and one draw needn't show every extreme that they name: energy_map is a permutation: every grid point 0 to 127 is held by exactly one slot.
All inputs are finite; a program needn't handle non-finite values.
Results may differ from a plain program's by a relative error of at most 0.0001.
Values sent between devices are 32-bit elements; how exact they have to be, the bound alone decides.
No kernel may reach another device: no remote copies, remote signals or barrier semaphores. Data moves between devices by JAX's collectives and lax.ppermute only.
A program may use at most 128 MiB of HBM per device.

v0:
```python
import math

import jax
import jax.numpy as jnp
from jax import lax
from jax.sharding import PartitionSpec as P

energy_floor = -2.0
energy_span = 4.0
broadening = 1.0
chemical = 0.0
thermal = 0.25


def from_partner(array, axis, apart):
    return lax.ppermute(array, axis, [(i, i ^ 1 << apart) for i in range(lax.axis_size(axis))])


def occupation(energy):
    return 1.0 / (1.0 + jnp.exp((energy - chemical) / thermal))


def cmatmul(left_pair, right_pair):

    def product(left_factor, right_factor):
        return jnp.dot(
            left_factor,
            right_factor,
            preferred_element_type=jnp.float32,
            precision=lax.Precision.HIGHEST,
        )

    return (
        product(left_pair[0], right_pair[0]) - product(left_pair[1], right_pair[1]),
        product(left_pair[0], right_pair[1]) + product(left_pair[1], right_pair[0]),
    )


def approx_inverse(mat_pair):
    mat_re, mat_im = mat_pair
    dimension = mat_re.shape[-1]
    diag_re = jnp.diagonal(mat_re)
    diag_im = jnp.diagonal(mat_im)
    magnitude = diag_re * diag_re + diag_im * diag_im
    recip_re = diag_re / magnitude
    recip_im = -diag_im / magnitude
    outer_re = recip_re[:, None] * recip_re[None, :] - recip_im[:, None] * recip_im[None, :]
    outer_im = recip_re[:, None] * recip_im[None, :] + recip_im[:, None] * recip_re[None, :]
    identity = jnp.eye(dimension, dtype=mat_re.dtype)
    first_re = 2.0 * identity * recip_re[None, :] - (outer_re * mat_re - outer_im * mat_im)
    first_im = 2.0 * identity * recip_im[None, :] - (outer_re * mat_im + outer_im * mat_re)
    applied = cmatmul((mat_re, mat_im), (first_re, first_im))
    second = cmatmul((first_re, first_im), applied)
    return (2.0 * first_re - second[0], 2.0 * first_im - second[1])


def spectral_blocks(hermitian, coupling, sigma_pair, energy):
    blocks = hermitian[0].shape[0]
    dimension = hermitian[0].shape[-1]
    identity = jnp.eye(dimension, dtype=hermitian[0].dtype)
    adjoint = (coupling[0].T, -coupling[1].T)

    def shifted(block_id):
        return (
            energy * identity - hermitian[0][block_id] - sigma_pair[0][block_id],
            broadening * identity - hermitian[1][block_id] - sigma_pair[1][block_id],
        )

    left_green = [approx_inverse(shifted(0))]
    block_id = 1
    coupled = cmatmul(cmatmul(adjoint, left_green[-1]), coupling)
    shifted_block = shifted(block_id)
    left_green.append(
        approx_inverse((shifted_block[0] - coupled[0], shifted_block[1] - coupled[1]))
    )
    full_green = [left_green[-1]]
    block_id = 0
    local_green = left_green[block_id]
    outgoing = cmatmul(local_green, coupling)
    incoming = cmatmul(adjoint, local_green)
    middle = cmatmul(cmatmul(outgoing, full_green[0]), incoming)
    full_green.insert(0, (local_green[0] + middle[0], local_green[1] + middle[1]))
    spec_re = jnp.stack([-(green[1] + green[1].T) for green in full_green])
    spec_im = jnp.stack([green[0] - green[0].T for green in full_green])
    return jnp.stack([spec_re, spec_im])


def phase_table(row_index, column_index, length):
    wrapped = row_index[:, None] * column_index[None, :] % length
    return wrapped.astype(jnp.float32) * (2.0 * math.pi / length)


def select_pair(condition, first_pair, second_pair):
    return (
        jnp.where(condition, first_pair[0], second_pair[0]),
        jnp.where(condition, first_pair[1], second_pair[1]),
    )


def times_conj(left_pair, right_pair):
    return (
        left_pair[0] * right_pair[0] + left_pair[1] * right_pair[1],
        left_pair[1] * right_pair[0] - left_pair[0] * right_pair[1],
    )


def times_plain(left_pair, right_pair):
    return (
        left_pair[0] * right_pair[0] - left_pair[1] * right_pair[1],
        left_pair[0] * right_pair[1] + left_pair[1] * right_pair[0],
    )


def add_pairs(first_pair, second_pair):
    return (first_pair[0] + second_pair[0], first_pair[1] + second_pair[1])


def on_device(hamiltonian, hopping, self_energy, screened, energy_map):
    local_slots = energy_map.shape[0]
    grid_index = lax.all_gather(energy_map, "energy", axis=0, tiled=True)
    slot_count = grid_index.shape[0]
    spacing = energy_span / slot_count
    blocks = hamiltonian.shape[1]
    block_order = hamiltonian.shape[-1]
    elements = blocks * block_order * block_order
    inter_flat = screened[0].reshape(local_slots, 2, elements)
    raw_re = hamiltonian[0, :, 0]
    raw_im = hamiltonian[0, :, 1]
    hermitian = (
        0.5 * (raw_re + jnp.swapaxes(raw_re, 1, 2)),
        0.5 * (raw_im - jnp.swapaxes(raw_im, 1, 2)),
    )
    coupling = (hopping[0, 0], hopping[0, 1])
    energies = energy_floor + spacing * energy_map.astype(jnp.float32)
    spectra = jnp.stack(
        [
            spectral_blocks(
                hermitian, coupling, (self_energy[0, 0, 0], self_energy[0, 0, 1]), energies[0]
            )
        ]
    )
    spec_flat = spectra.reshape(local_slots, 2, elements)
    length = 2 * slot_count
    frequency = jnp.arange(length, dtype=jnp.int32)
    forward_angle = phase_table(frequency, grid_index, length)
    forward = (jnp.cos(forward_angle), -jnp.sin(forward_angle))

    def transform(field_data):
        return cmatmul(forward, (field_data[:, 0], field_data[:, 1]))

    grid_points = jnp.arange(slot_count, dtype=jnp.int32)
    polar_angle = phase_table(grid_points, frequency, length)
    inverse_grid = (jnp.cos(polar_angle) / length, jnp.sin(polar_angle) / length)
    slot_angle = phase_table(grid_index, frequency, length)
    inverse_slot = (jnp.cos(slot_angle) / length, jnp.sin(slot_angle) / length)
    moment_id = lax.axis_index("mom")
    first_is_own = moment_id == 0
    inter_own = lax.all_to_all(inter_flat, "energy", split_axis=2, concat_axis=0, tiled=True)
    inter_other = from_partner(inter_own, "mom", 0)
    occupied = occupation(energies)[:, None, None]
    lesser_own, greater_own = (
        lax.all_to_all(occupied * spec_flat, "energy", split_axis=2, concat_axis=0, tiled=True),
        lax.all_to_all(
            (1.0 - occupied) * spec_flat, "energy", split_axis=2, concat_axis=0, tiled=True
        ),
    )
    lesser_other, greater_other = from_partner((lesser_own, greater_own), "mom", 0)
    lesser_a = transform(lesser_own)
    lesser_b = transform(lesser_other)
    greater_a = transform(greater_own)
    greater_b = transform(greater_other)
    inter_a = transform(inter_own)
    inter_b = transform(inter_other)
    greater_first = select_pair(first_is_own, greater_a, greater_b)
    greater_second = select_pair(first_is_own, greater_b, greater_a)
    lesser_first = select_pair(first_is_own, lesser_a, lesser_b)
    lesser_second = select_pair(first_is_own, lesser_b, lesser_a)
    polar_hat = add_pairs(times_conj(greater_first, lesser_a), times_conj(greater_second, lesser_b))
    sigma_hat = add_pairs(times_plain(lesser_first, inter_a), times_plain(lesser_second, inter_b))
    correlated = cmatmul(inverse_grid, polar_hat)
    polar = jnp.stack([spacing * correlated[1], -spacing * correlated[0]])
    convolved = cmatmul(inverse_slot, sigma_hat)
    sigma_elements = jnp.stack([-spacing * convolved[0], -spacing * convolved[1]], axis=1)
    returned = lax.all_to_all(sigma_elements, "energy", split_axis=0, concat_axis=2, tiled=True)
    new_sigma = returned.reshape(1, local_slots, 2, blocks, block_order, block_order)
    return (new_sigma, polar[None])


def solution(mesh):
    return jax.shard_map(
        on_device,
        mesh=mesh,
        in_specs=(
            P("mom", None, None, None, None),
            P("mom", None, None, None),
            P("mom", "energy", None, None, None, None),
            P("mom", "energy", None, None, None, None),
            P("energy"),
        ),
        out_specs=(P("mom", "energy", None, None, None, None), P("mom", None, None, "energy")),
        check_vma=False,
    )
```

profile of v0, /device:TPU:1, one launch (start us, length us, event | category | flops | bytes accessed | tf_op | source)
XLA Modules:
  0.0 815.0 jit_solution(4647081505366607363)
XLA Ops:
  5.3 1.2 gather_fusion.1
  6.6 1.2 gather_fusion
  19.3 1.2 gather_fusion.2
  31.5 23.9 %copy.82 = f32[1,2,32768]{1,0,2:T(1,128)} copy(f32[1,2,32768]{2,1,0:T(2,128)S(1)} %get-tuple-element.9) | data formatting | bytes 524288 | tf_op jit(solution)/shard_map/mul | solution.py:162
  55.9 146.6 %reduce = f32[32768,2]{1,0:T(8,128)} reduce(f32[32768,1,2]{2,1,0:T(1,128)} %bitcast.265, f32[]{:T(128)} %broadcast.639), dimensions={1}, to_apply=%bitcast.201.reduce_sub_computation | reduce | bytes 524292
  202.5 14.4 %reshape.654 = f32[128,1,512]{2,1,0:T(1,128)} reshape(f32[32768,2]{1,0:T(8,128)} %reduce) | data formatting | bytes 524288
  216.9 16.7 %all-to-all-start = ((f32[128,1,512]{2,1,0:T(1,128)}), f32[128,1,512]{2,1,0:T(1,128)S(1)}, u32[]{:S(2)}, u32[]{:S(2)}) async-start(f32[128,1,512]{2,1,0:T(1,128)} %reshape.654), calls=%async_computation | async-start | bytes 524288 | tf_op jit(solution)/shard_map/all_to_all | solution.py:162
  233.6 23.9 %copy.88 = f32[1,2,32768]{1,0,2:T(1,128)} copy(f32[1,2,32768]{2,1,0:T(2,128)S(1)} %get-tuple-element.8) | data formatting | bytes 524288 | tf_op jit(solution)/shard_map/mul | solution.py:164
  257.5 146.4 %reduce.2 = f32[32768,2]{1,0:T(8,128)} reduce(f32[32768,1,2]{2,1,0:T(1,128)} %bitcast.266, f32[]{:T(128)} %broadcast.639), dimensions={1}, to_apply=%bitcast.203.reduce_sub_computation | reduce | bytes 524292
  403.9 14.4 %reshape.656 = f32[128,1,512]{2,1,0:T(1,128)} reshape(f32[32768,2]{1,0:T(8,128)} %reduce.2) | data formatting | bytes 524288
  418.3 14.4 %all-to-all-start.3 = ((f32[128,1,512]{2,1,0:T(1,128)}), f32[128,1,512]{2,1,0:T(1,128)S(1)}, u32[]{:S(2)}, u32[]{:S(2)}) async-start(f32[128,1,512]{2,1,0:T(1,128)} %reshape.656), calls=%async_computation.3 | async-start | bytes 524288 | tf_op jit(solution)/shard_map/all_to_all | solution.py:163
  432.8 8.5 %copy.84 = f32[1,1,2,2,128,128]{2,5,4,3,1,0:T(8,128)} copy(f32[1,1,2,2,128,128]{5,4,3,2,1,0:T(8,128)S(1)} %copy-done) | data formatting | bytes 524288 | tf_op args[3]
  441.3 146.4 %reduce.4 = f32[32768,2]{1,0:T(8,128)} reduce(f32[32768,1,2]{2,1,0:T(1,128)} %bitcast.270, f32[]{:T(128)} %broadcast.639), dimensions={1}, to_apply=%bitcast.199.reduce_sub_computation | reduce | bytes 524292
  587.8 14.4 %reshape.652 = f32[128,1,512]{2,1,0:T(1,128)} reshape(f32[32768,2]{1,0:T(8,128)} %reduce.4) | data formatting | bytes 524288
  603.5 21.1 %all-reduce = s32[128]{0:T(128)S(1)} all-reduce(s32[128]{0:T(128)S(1)} %dynamic-update-slice), channel_id=1, replica_groups=mesh['energy'=128,'mom'=2] {'energy'}, use_global_device_ids=true, to_apply=%add | all-reduce | flops 128 | bytes 1024
  625.8 28.4 %reshape.655 = f32[32768,1,2]{2,1,0:T(1,128)} reshape(f32[128,512]{1,0:T(8,128)S(1)} %reduce.1) | data formatting | bytes 524288
  654.2 10.0 %copy.94 = f32[1,2,128,256]{3,2,1,0:T(8,128)S(1)} copy(f32[1,2,128,256]{1,3,2,0:T(8,128)} %bitcast.267) | data formatting | bytes 524288 | tf_op jit(solution)/shard_map/all_to_all | solution.py:162
  665.5 11.9 %all-to-all-start.1 = ((f32[128,1,512]{2,1,0:T(1,128)}), f32[128,1,512]{2,1,0:T(1,128)S(1)}, u32[]{:S(2)}, u32[]{:S(2)}) async-start(f32[128,1,512]{2,1,0:T(1,128)} %reshape.652), calls=%async_computation.1 | async-start | bytes 524288 | tf_op jit(solution)/shard_map/all_to_all | solution.py:158
  679.4 28.4 %reshape.657 = f32[32768,1,2]{2,1,0:T(1,128)} reshape(f32[128,512]{1,0:T(8,128)S(1)} %reduce.3) | data formatting | bytes 524288
  707.8 10.0 %copy.96 = f32[1,2,128,256]{3,2,1,0:T(8,128)S(1)} copy(f32[1,2,128,256]{1,3,2,0:T(8,128)} %bitcast.268) | data formatting | bytes 524288 | tf_op jit(solution)/shard_map/all_to_all | solution.py:163
  721.6 28.4 %reshape.653 = f32[32768,1,2]{2,1,0:T(1,128)} reshape(f32[128,512]{1,0:T(8,128)S(1)} %reduce.5) | data formatting | bytes 524288
  750.0 10.0 %copy.95 = f32[1,2,128,256]{3,2,1,0:T(8,128)S(1)} copy(f32[1,2,128,256]{1,3,2,0:T(8,128)} %bitcast.269) | data formatting | bytes 524288 | tf_op jit(solution)/shard_map/all_to_all | solution.py:158
  782.8 14.8 %all-to-all-start.2 = ((f32[128,2,256]{2,1,0:T(2,128)}), f32[128,2,256]{2,1,0:T(2,128)S(1)}, u32[]{:S(2)}, u32[]{:S(2)}) async-start(f32[128,2,256]{2,1,0:T(2,128)} %copy.86), calls=%async_computation.2 | async-start | bytes 524288 | tf_op jit(solution)/shard_map/all_to_all | solution.py:184
  801.5 12.6 %all-to-all-done.2 = f32[128,2,256]{2,1,0:T(2,128)S(1)} async-done(((f32[128,2,256]{2,1,0:T(2,128)}), f32[128,2,256]{2,1,0:T(2,128)S(1)}, u32[]{:S(2)}, u32[]{:S(2)}) %all-to-all-start.2) | async-done | bytes 262176 | tf_op jit(solution)/shard_map/all_to_all | solution.py:184
  (117 shorter events, 63.4 us)
Async XLA Ops:
  216.9 201.5 %all-to-all-start = ((f32[128,1,512]{2,1,0:T(1,128)}), f32[128,1,512]{2,1,0:T(1,128)S(1)}, u32[]{:S(2)}, u32[]{:S(2)}) async-start(f32[128,1,512]{2,1,0:T(1,128)} %reshape.654), calls=%async_computation | async-start | bytes 524288 | tf_op jit(solution)/shard_map/all_to_all | solution.py:162
  403.9 28.9 %copy-start = (f32[1,1,2,2,128,128]{5,4,3,2,1,0:T(8,128)S(1)}, f32[1,1,2,2,128,128]{5,4,3,2,1,0:T(8,128)}, u32[]{:S(2)}) copy-start(f32[1,1,2,2,128,128]{5,4,3,2,1,0:T(8,128)} %param.8) | copy-start | bytes 786436
  418.3 247.1 %all-to-all-start.3 = ((f32[128,1,512]{2,1,0:T(1,128)}), f32[128,1,512]{2,1,0:T(1,128)S(1)}, u32[]{:S(2)}, u32[]{:S(2)}) async-start(f32[128,1,512]{2,1,0:T(1,128)} %reshape.656), calls=%async_computation.3 | async-start | bytes 524288 | tf_op jit(solution)/shard_map/all_to_all | solution.py:163
  587.8 14.4 %copy-start.1 = (u32[256]{0:T(256)S(1)}, u32[256]{0:T(256)}, u32[]{:S(2)}) copy-start(u32[256]{0:T(256)} %constant.134) | copy-start | bytes 3076
  664.1 106.9 %collective-permute-start = (f32[128,2,256]{2,0,1:T(8,128)S(1)}, f32[128,2,256]{2,0,1:T(8,128)S(1)}, u32[]{:S(2)}, u32[]{:S(2)}) collective-permute-start(f32[128,2,256]{2,0,1:T(8,128)S(1)} %bitcast.271), channel_id=1, source_target_pairs={{0,1},{1,0},{2,3},{3,2},{4,5},{5,4},{6,7},{7,6},{8,9},{9,8},{10,11... | collective-permute-start | bytes 786440 | tf_op jit(solution)/shard_map/ppermute | solution.py:16
  665.5 55.0 %all-to-all-start.1 = ((f32[128,1,512]{2,1,0:T(1,128)}), f32[128,1,512]{2,1,0:T(1,128)S(1)}, u32[]{:S(2)}, u32[]{:S(2)}) async-start(f32[128,1,512]{2,1,0:T(1,128)} %reshape.652), calls=%async_computation.1 | async-start | bytes 524288 | tf_op jit(solution)/shard_map/all_to_all | solution.py:158
  717.7 49.9 %collective-permute-start.2 = (f32[128,2,256]{2,0,1:T(8,128)S(1)}, f32[128,2,256]{2,0,1:T(8,128)S(1)}, u32[]{:S(2)}, u32[]{:S(2)}) collective-permute-start(f32[128,2,256]{2,0,1:T(8,128)S(1)} %bitcast.276), channel_id=1, source_target_pairs={{0,1},{1,0},{2,3},{3,2},{4,5},{5,4},{6,7},{7,6},{8,9},{9,8},{10,11... | collective-permute-start | bytes 786440 | tf_op jit(solution)/shard_map/ppermute | solution.py:16
  760.0 9.3 %collective-permute-start.1 = (f32[128,2,256]{2,0,1:T(8,128)S(1)}, f32[128,2,256]{2,0,1:T(8,128)S(1)}, u32[]{:S(2)}, u32[]{:S(2)}) collective-permute-start(f32[128,2,256]{2,0,1:T(8,128)S(1)} %bitcast.281), channel_id=1, source_target_pairs={{0,1},{1,0},{2,3},{3,2},{4,5},{5,4},{6,7},{7,6},{8,9},{9,8},{10,11... | collective-permute-start | bytes 786440 | tf_op jit(solution)/shard_map/ppermute | solution.py:16
  782.8 31.3 %all-to-all-start.2 = ((f32[128,2,256]{2,1,0:T(2,128)}), f32[128,2,256]{2,1,0:T(2,128)S(1)}, u32[]{:S(2)}, u32[]{:S(2)}) async-start(f32[128,2,256]{2,1,0:T(2,128)} %copy.86), calls=%async_computation.2 | async-start | bytes 524288 | tf_op jit(solution)/shard_map/all_to_all | solution.py:184
where the time goes:
time: 824 us; the launch traced here: 815 us
  other arithmetic  447 us (54%)
  local copies, waits for them, and re-layouts  225 us (27%)
  starting transfers between devices  60.1 us (7%)
  matrix products  46.8 us (6%)
  blocking collectives  21.1 us (3%)
  waiting for transfers between devices  12.6 us (2%)
    unnamed x3, other arithmetic  439 us
    unnamed x17, local copies, waits for them, and re-layouts  139 us
    dot_general x68, matrix products, product(): jnp.dot(left_factor, right_factor, preferred_element_type=jnp.float32, pr...  46.8 us
    mul x1, local copies, waits for them, and re-layouts, on_device(): occupied * spec_flat  23.9 us
    mul x1, local copies, waits for them, and re-layouts, on_device(): (1.0 - occupied) * spec_flat  23.9 us
    unnamed x1, blocking collectives  21.1 us
    all_to_all x1, starting transfers between devices, on_device(): lax.all_to_all(occupied * spec_flat, 'energy', split_axis=2, concat_axis=...  16.7 us
  transfers between devices with their start and end apart: 7, of which 1 were waited for; matrix products, arithmetic and copies ran while one was open for 60% of the time, Pallas kernels for 0%

commit v1 on v0

v1 whole, which is shorter than its diff:
```python
import math

import jax
import jax.numpy as jnp
import numpy as np
from jax import lax
from jax.experimental import pallas as pl
from jax.experimental.pallas import tpu as pltpu
from jax.sharding import PartitionSpec as P

energy_floor = -2.0
energy_span = 4.0
broadening = 1.0
chemical = 0.0
thermal = 0.25

chunk_rows = 4
inter_rows = 5


def from_partner(array, axis):
    return lax.ppermute(array, axis, [(i, i ^ 1) for i in range(lax.axis_size(axis))])


def occupation(energy):
    return 1.0 / (1.0 + jnp.exp((energy - chemical) / thermal))


def halves(value):
    high = value.astype(jnp.bfloat16)
    return high, (value - high.astype(jnp.float32)).astype(jnp.bfloat16)


def dot(left, right):
    return jnp.dot(left, right, preferred_element_type=jnp.float32)


def dot3(left, right):
    return dot(left[0], right[0]) + (dot(left[0], right[1]) + dot(left[1], right[0]))


def left_form(pair):
    return halves(jnp.concatenate(pair, axis=1))


def right_form(pair):
    re, im = halves(pair[0]), halves(pair[1])
    return tuple(
        jnp.concatenate(
            [jnp.concatenate([re[n], im[n]], axis=1), jnp.concatenate([-im[n], re[n]], axis=1)],
            axis=0,
        )
        for n in range(2)
    )


def cproduct(left, right):
    result = dot3(left, right)
    order = result.shape[0]
    return result[:, :order], result[:, order:]


def approx_inverse(mat_re, mat_im, eye):
    def diagonal(values, axis):
        return jnp.sum(jnp.where(eye, values, 0.0), axis=axis, keepdims=True)

    def reciprocal(axis):
        diag_re, diag_im = diagonal(mat_re, axis), diagonal(mat_im, axis)
        magnitude = diag_re * diag_re + diag_im * diag_im
        return diag_re / magnitude, -diag_im / magnitude

    col_re, col_im = reciprocal(1)
    row_re, row_im = reciprocal(0)
    outer_re = col_re * row_re - col_im * row_im
    outer_im = col_re * row_im + col_im * row_re
    first_re = jnp.where(eye, 2.0 * row_re, 0.0) - (outer_re * mat_re - outer_im * mat_im)
    first_im = jnp.where(eye, 2.0 * row_im, 0.0) - (outer_re * mat_im + outer_im * mat_re)
    first = (first_re, first_im)
    applied = cproduct(left_form((mat_re, mat_im)), right_form(first))
    second = cproduct(left_form(first), right_form(applied))
    return 2.0 * first_re - second[0], 2.0 * first_im - second[1]


def pack_kernel(map_ref, screened_ref, out_ref):
    blocks, order = screened_ref.shape[3], screened_ref.shape[4]
    half = order // 2
    for part in range(2):
        for block in range(blocks):
            for low in range(2):
                start = block * half * inter_rows + part * 2 + low
                out_ref[pl.ds(start, half, stride=inter_rows), :] = screened_ref[
                    0, 0, part, block, pl.ds(low, half, stride=2), :
                ]
    pieces = blocks * half
    index = jnp.full((pieces, order), map_ref[0], jnp.int32).astype(jnp.float32)
    out_ref[pl.ds(4, pieces, stride=inter_rows), :] = index


def green_kernel(spacing, map_ref, ham_ref, hop_ref, self_ref, out_ref, spec_ref):
    order = ham_ref.shape[3]
    half = order // 2
    rows = lax.broadcasted_iota(jnp.int32, (order, order), 0)
    cols = lax.broadcasted_iota(jnp.int32, (order, order), 1)
    eye = rows == cols
    index = jnp.full((order, order), map_ref[0], jnp.int32).astype(jnp.float32)
    energy = energy_floor + spacing * index

    def shifted(block):
        raw_re, raw_im = ham_ref[0, block, 0], ham_ref[0, block, 1]
        herm_re = 0.5 * (raw_re + raw_re.T)
        herm_im = 0.5 * (raw_im - raw_im.T)
        return (
            jnp.where(eye, energy, 0.0) - herm_re - self_ref[0, 0, 0, block],
            jnp.where(eye, broadening, 0.0) - herm_im - self_ref[0, 0, 1, block],
        )

    hop = (hop_ref[0, 0], hop_ref[0, 1])
    adjoint = (hop[0].T, -hop[1].T)
    hop_right = right_form(hop)
    local = approx_inverse(*shifted(0), eye)
    incoming = cproduct(left_form(adjoint), right_form(local))
    outgoing = cproduct(left_form(local), hop_right)
    coupled = cproduct(left_form(incoming), hop_right)
    last = shifted(1)
    green = approx_inverse(last[0] - coupled[0], last[1] - coupled[1], eye)
    middle = cproduct(left_form(outgoing), right_form(green))
    middle = cproduct(left_form(middle), right_form(incoming))
    full = ((local[0] + middle[0], local[1] + middle[1]), green)
    for block in range(2):
        spec_ref[0] = -(full[block][1] + full[block][1].T)
        spec_ref[1] = full[block][0] - full[block][0].T
        for part in range(2):
            for low in range(2):
                start = block * half * chunk_rows + part * 2 + low
                out_ref[pl.ds(start, half, stride=chunk_rows), :] = spec_ref[
                    part, pl.ds(low, half, stride=2), :
                ]


def gather_field(ref, stride, scale=None):
    slots = ref.shape[0] // stride

    def part(row):
        values = ref[pl.ds(row, slots, stride=stride), :]
        return values if scale is None else scale * values

    return jnp.concatenate(
        [
            jnp.concatenate([part(0), part(1)], axis=1),
            jnp.concatenate([part(2), part(3)], axis=1),
        ],
        axis=0,
    )


def table_kernel(
    spacing, own_ref, other_ref, wave_ref, wave_t_ref, fwd_ref, inv_ref, hat_ref, occ_ref
):
    slots = occ_ref.shape[0]
    index = own_ref[pl.ds(4, slots, stride=inter_rows), :]
    occ_ref[...] = occupation(energy_floor + spacing * index)
    grid = lax.broadcasted_iota(jnp.int32, index.shape, 1).astype(jnp.float32)
    chosen = jnp.where(index == grid, 1.0, 0.0).astype(jnp.bfloat16)
    contract = (((1,), (1,)), ((), ()))
    for n in range(2):
        wave = [
            lax.dot_general(
                wave_ref[n, part], chosen, contract, preferred_element_type=jnp.float32
            ).astype(jnp.bfloat16)
            for part in range(2)
        ]
        fwd_ref[n] = jnp.concatenate(
            [
                jnp.concatenate([wave[0], -wave[1]], axis=1),
                jnp.concatenate([wave[1], wave[0]], axis=1),
            ],
            axis=0,
        )
        turned = [dot(chosen, wave_t_ref[n, part]).astype(jnp.bfloat16) for part in range(2)]
        inv_ref[n] = jnp.concatenate(
            [
                jnp.concatenate([turned[0], turned[1]], axis=1),
                jnp.concatenate([-turned[1], turned[0]], axis=1),
            ],
            axis=0,
        )
    forward = (fwd_ref[0], fwd_ref[1])
    hat_ref[0] = dot3(forward, halves(gather_field(own_ref, inter_rows)))
    hat_ref[1] = dot3(forward, halves(gather_field(other_ref, inter_rows)))


def sigma_kernel(
    spacing, mom_ref, own_ref, other_ref, occ_ref, fwd_ref, inv_ref, inter_ref, send_ref, hat_ref
):
    slots = occ_ref.shape[0]
    length = 2 * slots
    forward = (fwd_ref[0], fwd_ref[1])
    occupied = occ_ref[...]
    hat_ref[0] = dot3(forward, halves(gather_field(own_ref, chunk_rows, occupied)))
    hat_ref[1] = dot3(forward, halves(gather_field(other_ref, chunk_rows, occupied)))
    moment = mom_ref[0]
    sum_re = sum_im = 0.0
    for n, source in enumerate((moment, 1 - moment)):
        left_re, left_im = hat_ref[source, :length], hat_ref[source, length:]
        right_re, right_im = inter_ref[n, :length], inter_ref[n, length:]
        sum_re += left_re * right_re - left_im * right_im
        sum_im += left_re * right_im + left_im * right_re
    inverse = (inv_ref[0], inv_ref[1])
    result = dot3(inverse, halves(jnp.concatenate([sum_re, sum_im], axis=0)))
    result = result * (-spacing / length)
    for part in range(2):
        for low in range(2):
            send_ref[pl.ds(part * 2 + low, slots, stride=chunk_rows), :] = result[
                part * slots : (part + 1) * slots, low * 128 : (low + 1) * 128
            ]


def polar_kernel(
    spacing, mom_ref, own_ref, other_ref, occ_ref, fwd_ref, back_ref, hat_ref, out_ref, great_ref
):
    slots = occ_ref.shape[0]
    length = 2 * slots
    forward = (fwd_ref[0], fwd_ref[1])
    empty = 1.0 - occ_ref[...]
    great_ref[0] = dot3(forward, halves(gather_field(own_ref, chunk_rows, empty)))
    great_ref[1] = dot3(forward, halves(gather_field(other_ref, chunk_rows, empty)))
    moment = mom_ref[0]
    sum_re = sum_im = 0.0
    for n, source in enumerate((moment, 1 - moment)):
        left_re, left_im = great_ref[source, :length], great_ref[source, length:]
        right_re, right_im = hat_ref[n, :length], hat_ref[n, length:]
        sum_re += left_re * right_re + left_im * right_im
        sum_im += left_im * right_re - left_re * right_im
    back = (back_ref[0], back_ref[1])
    result = dot3(back, halves(jnp.concatenate([sum_re, sum_im], axis=0)))
    out_ref[0, 0] = result[slots:] * (spacing / length)
    out_ref[0, 1] = result[:slots] * (-spacing / length)


def unpack_kernel(recv_ref, out_ref):
    blocks, order = out_ref.shape[3], out_ref.shape[4]
    half = order // 2
    for part in range(2):
        for block in range(blocks):
            for low in range(2):
                start = block * half * chunk_rows + part * 2 + low
                out_ref[0, 0, part, block, pl.ds(low, half, stride=2), :] = recv_ref[
                    pl.ds(start, half, stride=chunk_rows), :
                ]


def call(kernel, outs, scalars, name, scratch=()):
    vmem = pl.BlockSpec(memory_space=pltpu.VMEM)
    smem = pl.BlockSpec(memory_space=pltpu.SMEM)

    def run(*operands):
        return pl.pallas_call(
            kernel,
            out_shape=outs,
            in_specs=[smem] * scalars + [vmem] * (len(operands) - scalars),
            out_specs=jax.tree.map(lambda _: vmem, outs),
            scratch_shapes=list(scratch),
            name=name,
        )(*operands)

    return run


def exchange(rows, count):
    chunks = rows.reshape(count, rows.shape[0] // count, rows.shape[1])
    moved = lax.all_to_all(chunks, "energy", split_axis=0, concat_axis=0, tiled=True)
    return moved.reshape(rows.shape)


def split_table(table):
    high = table.astype(np.float32).astype(jnp.bfloat16)
    low = (table - high.astype(np.float64)).astype(np.float32).astype(jnp.bfloat16)
    return np.stack([high, low])


def on_device(hamiltonian, hopping, self_energy, screened, energy_map):
    slots = lax.axis_size("energy")
    spacing = energy_span / slots
    length = 2 * slots
    order = hamiltonian.shape[-1]
    angle = (np.arange(length)[:, None] * np.arange(slots)[None, :] % length) * (
        2.0 * math.pi / length
    )
    wave = np.stack([np.cos(angle), -np.sin(angle)])
    wave_t = np.swapaxes(wave, 1, 2)
    back = np.block([[wave_t[0], wave_t[1]], [-wave_t[1], wave_t[0]]])
    wave, wave_t, back = (jnp.asarray(split_table(t)) for t in (wave, wave_t, back))

    def f32(*shape):
        return jax.ShapeDtypeStruct(shape, jnp.float32)

    def b16(*shape):
        return jax.ShapeDtypeStruct(shape, jnp.bfloat16)

    moment = lax.axis_index("mom").astype(jnp.int32).reshape(1)
    packed = call(pack_kernel, f32(slots * inter_rows, order), 1, "pack")(energy_map, screened)
    packed = packed.reshape(slots, 1, inter_rows * order)
    inter_own = lax.all_to_all(packed, "energy", split_axis=0, concat_axis=0, tiled=True)
    inter_own = inter_own.reshape(slots * inter_rows, order)
    inter_other = from_partner(inter_own, "mom")
    spectrum = call(
        lambda *refs: green_kernel(spacing, *refs),
        f32(slots * chunk_rows, order),
        1,
        "green",
        [pltpu.VMEM((2, order, order), jnp.float32)],
    )(energy_map, hamiltonian, hopping, self_energy)
    own = exchange(spectrum, slots)
    forward, inverse, inter_hat, occupied = call(
        lambda *refs: table_kernel(spacing, *refs),
        (
            b16(2, 2 * length, 2 * slots),
            b16(2, 2 * slots, 2 * length),
            f32(2, 2 * length, 2 * order),
            f32(slots, order),
        ),
        0,
        "tables",
    )(inter_own, inter_other, wave, wave_t)
    own, occupied = lax.optimization_barrier((own, occupied))
    other = from_partner(own, "mom")
    send, lesser_hat = call(
        lambda *refs: sigma_kernel(spacing, *refs),
        (f32(slots * chunk_rows, order), f32(2, 2 * length, 2 * order)),
        1,
        "sigma",
    )(moment, own, other, occupied, forward, inverse, inter_hat)
    returned = exchange(send, slots)
    polar = call(
        lambda *refs: polar_kernel(spacing, *refs),
        f32(1, 2, slots, 2 * order),
        1,
        "polar",
        [pltpu.VMEM((2, 2 * length, 2 * order), jnp.float32)],
    )(moment, own, other, occupied, forward, back, lesser_hat)
    new_sigma = call(unpack_kernel, f32(*screened.shape), 0, "unpack")(returned)
    return (new_sigma, polar)


def solution(mesh):
    return jax.shard_map(
        on_device,
        mesh=mesh,
        in_specs=(
            P("mom", None, None, None, None),
            P("mom", None, None, None),
            P("mom", "energy", None, None, None, None),
            P("mom", "energy", None, None, None, None),
            P("energy"),
        ),
        out_specs=(P("mom", "energy", None, None, None, None), P("mom", None, None, "energy")),
        check_vma=False,
    )
```

time: 824 us -> 105 us (0.13); the launches traced: 815 us -> 104 us
  other arithmetic: 447 us -> 0 us
  local copies, waits for them, and re-layouts: 225 us -> 2.12 us
  matrix products: 46.8 us -> 0 us
  waiting for transfers between devices: 12.6 us -> 46.3 us
  starting transfers between devices: 60.1 us -> 36.4 us
  blocking collectives: 21.1 us -> 0 us
  Pallas kernels: 0 us -> 18.1 us
    unnamed x3 -> x0, other arithmetic: 439 us -> none
    unnamed x17 -> x10, local copies, waits for them, and re-layouts: 139 us -> 2.12 us
    mul x2 -> x0, local copies, waits for them, and re-layouts: 47.7 us -> none  [the longest x1 23.9 us: on_device(): occupied * spec_flat]
    dot_general x68 -> x0, matrix products: 46.8 us -> none  [product(): jnp.dot(left_factor, right_factor, preferred_element_type=jnp.float32, pr...]
    all_to_all x4 -> x0, local copies, waits for them, and re-layouts: 29.9 us -> none  [the longest x1 9.95 us: on_device(): lax.all_to_all(occupied * spec_flat, 'energy', split_axis=2, concat_axis=...]
    all_to_all x4 -> x3, starting transfers between devices: 57.8 us -> 35.5 us  [the longest x2 19.1 us: exchange(): lax.all_to_all(chunks, 'energy', split_axis=0, concat_axis=0, tiled=True)]
    unnamed x1 -> x0, blocking collectives: 21.1 us -> none
    pallas_call x0 -> x6, Pallas kernels: none -> 18.1 us  [run(): pl.pallas_call(kernel, out_shape=outs, in_specs=[smem] * scalars + [vmem]...]
  transfers between devices with their start and end apart: 7 -> 5, of which waited for: 1 -> 5; matrix products, arithmetic and copies ran while one was open for 60% -> 0% of each run, Pallas kernels for 0% -> 10%
where the time goes in v1:
time: 105 us; the launch traced here: 104 us
  waiting for transfers between devices  46.3 us (44%)
  starting transfers between devices  36.4 us (35%)
  Pallas kernels  18.1 us (17%)
  local copies, waits for them, and re-layouts  2.12 us (2%)
  between operations  1.31 us (1%)
    all_to_all x2, starting transfers between devices, exchange(): lax.all_to_all(chunks, 'energy', split_axis=0, concat_axis=0, tiled=True)  19.1 us
    pallas_call x6, Pallas kernels, run(): pl.pallas_call(kernel, out_shape=outs, in_specs=[smem] * scalars + [vmem]...  18.1 us
    ppermute x2, waiting for transfers between devices, from_partner(): lax.ppermute(array, axis, [(i, i ^ 1) for i in range(lax.axis_size(axis))])  17.7 us
    all_to_all x1, starting transfers between devices, on_device(): lax.all_to_all(packed, 'energy', split_axis=0, concat_axis=0, tiled=True)  16.4 us
    all_to_all x2, waiting for transfers between devices, exchange(): lax.all_to_all(chunks, 'energy', split_axis=0, concat_axis=0, tiled=True)  14.7 us
    all_to_all x1, waiting for transfers between devices, on_device(): lax.all_to_all(packed, 'energy', split_axis=0, concat_axis=0, tiled=True)  13.9 us
    unnamed x10, local copies, waits for them, and re-layouts  2.12 us
  transfers between devices with their start and end apart: 5, of which 5 were waited for; matrix products, arithmetic and copies ran while one was open for 0% of the time, Pallas kernels for 10%

profile of v1, /device:TPU:1, one launch (start us, length us, event | category | flops | bytes accessed | tf_op | source)
XLA Modules:
  0.0 104.3 jit_solution(1638170005716409327)
XLA Ops:
  1.3 1.7 %pack.1 = f32[640,128]{1,0:T(8,128)} custom-call(s32[1]{0:T(128)S(6)} %copy.11.refs_0_.map_ref, f32[1,1,2,2,128,128]{5,4,3,2,1,0:T(8,128)} %screened_ref.1), custom_call_target="tpu_custom_call" | custom-call | tf_op jit(solution)/shard_map/pack/pallas_call | solution.py:257
  3.0 16.4 %all-to-all-start.1 = ((f32[128,1,640]{2,1,0:T(1,128)}), f32[128,1,640]{2,1,0:T(1,128)S(1)}, u32[]{:S(2)}, u32[]{:S(2)}) async-start(f32[128,1,640]{2,1,0:T(1,128)} %bitcast.12), calls=%async_computation.1 | async-start | bytes 655360 | tf_op jit(solution)/shard_map/all_to_all | solution.py:303
  19.4 4.0 %green.1 = f32[512,128]{1,0:T(8,128)} custom-call(s32[1]{0:T(128)S(6)} %copy.11.refs_0_.map_ref, f32[1,2,2,128,128]{4,3,2,1,0:T(8,128)} %refs_1_.1, f32[1,2,128,128]{3,2,1,0:T(8,128)} %refs_2_.2, f32[1,1,2,2,128,128]{5,4,3,2,1,0:T(8,128)} %refs_3_.2), custom_call_target="tpu_custom_call" | custom-call | tf_op jit(solution)/shard_map/green/pallas_call | solution.py:257
  23.4 13.9 %all-to-all-done.1 = f32[128,1,640]{2,1,0:T(1,128)S(1)} async-done(((f32[128,1,640]{2,1,0:T(1,128)}), f32[128,1,640]{2,1,0:T(1,128)S(1)}, u32[]{:S(2)}, u32[]{:S(2)}) %all-to-all-start.1) | async-done | bytes 327712 | tf_op jit(solution)/shard_map/all_to_all | solution.py:303
  37.3 0.0 copy-start.1
  37.3 5.6 %all-to-all-start = ((f32[128,4,128]{2,1,0:T(4,128)}), f32[128,4,128]{2,1,0:T(4,128)S(1)}, u32[]{:S(2)}, u32[]{:S(2)}) async-start(f32[128,4,128]{2,1,0:T(4,128)} %bitcast.13), calls=%async_computation | async-start | bytes 524288 | tf_op jit(solution)/shard_map/all_to_all | solution.py:271
  42.9 0.5 collective-permute-start
  43.4 10.6 %collective-permute-done.refs_1_ = f32[640,128]{1,0:T(8,128)S(1)} collective-permute-done((f32[640,128]{1,0:T(8,128)S(1)}, f32[640,128]{1,0:T(8,128)S(1)}, u32[]{:S(2)}, u32[]{:S(2)}) %collective-permute-start) | collective-permute-done | bytes 327712 | tf_op jit(solution)/shard_map/ppermute | solution.py:22
  54.0 0.0 copy-done.1
  54.0 0.0 copy-start.4
  54.0 0.7 copy-done.4
  54.7 3.0 %tables.1 = (bf16[2,512,256]{2,1,0:T(8,128)(2,1)}, bf16[2,256,512]{2,1,0:T(8,128)(2,1)}, f32[2,512,256]{2,1,0:T(8,128)}, f32[128,128]{1,0:T(8,128)}) custom-call(f32[640,128]{1,0:T(8,128)} %bitcast.11, f32[640,128]{1,0:T(8,128)} %copy-done.4, bf16[2,2,256,128]{3,2,1,0:T(8,128)(2,1)} %constant.10.clone.refs_2_, bf16[2,2,128,256]{3,2,1,0:T(8,128)(2,1)} %constant.11.clone.refs_3_), custom_call_target="tpu_custom_call" | custom-call | tf_op jit(solution)/shard_map/tables/pallas_call | solution.py:257
  57.7 1.9 %all-to-all-done = f32[128,4,128]{2,1,0:T(4,128)S(1)} async-done(((f32[128,4,128]{2,1,0:T(4,128)}), f32[128,4,128]{2,1,0:T(4,128)S(1)}, u32[]{:S(2)}, u32[]{:S(2)}) %all-to-all-start) | async-done | bytes 262176 | tf_op jit(solution)/shard_map/all_to_all | solution.py:271
  59.6 0.0 copy-start
  59.6 0.4 collective-permute-start.1
  60.0 7.1 %collective-permute-done.1.refs_2_ = f32[512,128]{1,0:T(8,128)S(1)} collective-permute-done((f32[512,128]{1,0:T(8,128)S(1)}, f32[512,128]{1,0:T(8,128)S(1)}, u32[]{:S(2)}, u32[]{:S(2)}) %collective-permute-start.1) | collective-permute-done | bytes 262176 | tf_op jit(solution)/shard_map/ppermute | solution.py:22
  67.1 0.0 copy-done
  67.1 0.7 copy-done.2
  67.8 3.9 %sigma.1 = (f32[512,128]{1,0:T(8,128)}, f32[2,512,256]{2,1,0:T(8,128)}) custom-call(s32[1]{0:T(128)} %bitcast.refs_0_, f32[512,128]{1,0:T(8,128)} %bitcast.8, f32[512,128]{1,0:T(8,128)} %copy-done.2, f32[128,128]{1,0:T(8,128)} %get-tuple-element.12.refs_3_, bf16[2,512,256]{2,1,0:T(8,128)(2,1)} %get-tuple-element.13.refs_4_, ...), custom_call_target="tpu_custom_call" | custom-call | tf_op jit(solution)/shard_map/sigma/pallas_call | solution.py:257
  71.7 13.6 %all-to-all-start.2 = ((f32[128,4,128]{2,1,0:T(4,128)}), f32[128,4,128]{2,1,0:T(4,128)S(1)}, u32[]{:S(2)}, u32[]{:S(2)}) async-start(f32[128,4,128]{2,1,0:T(4,128)} %bitcast.15), calls=%async_computation.2 | async-start | bytes 524288 | tf_op jit(solution)/shard_map/all_to_all | solution.py:271
  85.3 3.9 %polar.1 = f32[1,2,128,256]{3,2,1,0:T(8,128)} custom-call(s32[1]{0:T(128)} %bitcast.refs_0_, f32[512,128]{1,0:T(8,128)} %bitcast.9, f32[512,128]{1,0:T(8,128)} %copy-done.2, f32[128,128]{1,0:T(8,128)} %get-tuple-element.12.refs_3_, bf16[2,512,256]{2,1,0:T(8,128)(2,1)} %get-tuple-element.13.refs_4_, bf16[2,256,512]{2,1,0:T(8,128)(2,1)} %constant.12.clone.refs_5_, ...), custom_call_target="tpu_custom_call" | custom-call | tf_op jit(solution)/shard_map/polar/pallas_call | solution.py:257
  89.1 12.8 %all-to-all-done.2 = f32[128,4,128]{2,1,0:T(4,128)S(1)} async-done(((f32[128,4,128]{2,1,0:T(4,128)}), f32[128,4,128]{2,1,0:T(4,128)S(1)}, u32[]{:S(2)}, u32[]{:S(2)}) %all-to-all-start.2) | async-done | bytes 262176 | tf_op jit(solution)/shard_map/all_to_all | solution.py:271
  101.9 0.7 copy-done.3
  102.6 1.7 %unpack.1 = f32[1,1,2,2,128,128]{5,4,3,2,1,0:T(8,128)} custom-call(f32[512,128]{1,0:T(8,128)} %bitcast.14), custom_call_target="tpu_custom_call" | custom-call | tf_op jit(solution)/shard_map/unpack/pallas_call | solution.py:257
  (2 shorter events, 0.0 us)
Async XLA Ops:
  3.0 34.3 %all-to-all-start.1 = ((f32[128,1,640]{2,1,0:T(1,128)}), f32[128,1,640]{2,1,0:T(1,128)S(1)}, u32[]{:S(2)}, u32[]{:S(2)}) async-start(f32[128,1,640]{2,1,0:T(1,128)} %bitcast.12), calls=%async_computation.1 | async-start | bytes 655360 | tf_op jit(solution)/shard_map/all_to_all | solution.py:303
  37.3 16.7 %copy-start.1 = (f32[128,1,640]{2,1,0:T(1,128)}, f32[128,1,640]{2,1,0:T(1,128)S(1)}, u32[]{:S(2)}) copy-start(f32[128,1,640]{2,1,0:T(1,128)S(1)} %all-to-all-done.1) | copy-start | bytes 983044
  37.3 22.3 %all-to-all-start = ((f32[128,4,128]{2,1,0:T(4,128)}), f32[128,4,128]{2,1,0:T(4,128)S(1)}, u32[]{:S(2)}, u32[]{:S(2)}) async-start(f32[128,4,128]{2,1,0:T(4,128)} %bitcast.13), calls=%async_computation | async-start | bytes 524288 | tf_op jit(solution)/shard_map/all_to_all | solution.py:271
  42.9 11.1 %collective-permute-start = (f32[640,128]{1,0:T(8,128)S(1)}, f32[640,128]{1,0:T(8,128)S(1)}, u32[]{:S(2)}, u32[]{:S(2)}) collective-permute-start(f32[640,128]{1,0:T(8,128)S(1)} %bitcast.10), channel_id=1, source_target_pairs={{0,1},{1,0},{2,3},{3,2},{4,5},{5,4},{6,7},{7,6},{8,9},{9,8},{10,11... | collective-permute-start | bytes 983048 | tf_op jit(solution)/shard_map/ppermute | solution.py:22
  54.0 0.7 copy-start.4
  59.6 7.5 %copy-start = (f32[128,4,128]{2,1,0:T(4,128)}, f32[128,4,128]{2,1,0:T(4,128)S(1)}, u32[]{:S(2)}) copy-start(f32[128,4,128]{2,1,0:T(4,128)S(1)} %all-to-all-done) | copy-start | bytes 786436
  59.6 7.5 %collective-permute-start.1 = (f32[512,128]{1,0:T(8,128)S(1)}, f32[512,128]{1,0:T(8,128)S(1)}, u32[]{:S(2)}, u32[]{:S(2)}) collective-permute-start(f32[512,128]{1,0:T(8,128)S(1)} %bitcast.7), channel_id=1, source_target_pairs={{0,1},{1,0},{2,3},{3,2},{4,5},{5,4},{6,7},{7,6},{8,9},{9,8},{10,11... | collective-permute-start | bytes 786440 | tf_op jit(solution)/shard_map/ppermute | solution.py:22
  67.1 0.7 copy-start.2
  71.7 30.2 %all-to-all-start.2 = ((f32[128,4,128]{2,1,0:T(4,128)}), f32[128,4,128]{2,1,0:T(4,128)S(1)}, u32[]{:S(2)}, u32[]{:S(2)}) async-start(f32[128,4,128]{2,1,0:T(4,128)} %bitcast.15), calls=%async_computation.2 | async-start | bytes 524288 | tf_op jit(solution)/shard_map/all_to_all | solution.py:271
  101.9 0.7 copy-start.3

commit v2 on v1

v2 whole, which is shorter than its diff:
```python
import math

import jax
import jax.numpy as jnp
import numpy as np
from jax import lax
from jax.experimental import pallas as pl
from jax.experimental.pallas import tpu as pltpu
from jax.sharding import PartitionSpec as P

energy_floor = -2.0
energy_span = 4.0
broadening = 1.0
chemical = 0.0
thermal = 0.25

field_rows = 5


def from_partner(array, axis):
    return lax.ppermute(array, axis, [(i, i ^ 1) for i in range(lax.axis_size(axis))])


def occupation(energy):
    return 1.0 / (1.0 + jnp.exp((energy - chemical) / thermal))


def halves(value):
    high = value.astype(jnp.bfloat16)
    return high, (value - high.astype(jnp.float32)).astype(jnp.bfloat16)


def dot(left, right):
    return jnp.dot(left, right, preferred_element_type=jnp.float32)


def dot3(left, right):
    return dot(left[0], right[0]) + (dot(left[0], right[1]) + dot(left[1], right[0]))


def left_form(pair):
    return halves(jnp.concatenate(pair, axis=1))


def right_form(pair):
    re, im = halves(pair[0]), halves(pair[1])
    return tuple(
        jnp.concatenate(
            [jnp.concatenate([re[n], im[n]], axis=1), jnp.concatenate([-im[n], re[n]], axis=1)],
            axis=0,
        )
        for n in range(2)
    )


def cproduct(left, right):
    result = dot3(left, right)
    order = result.shape[0]
    return result[:, :order], result[:, order:]


def approx_inverse(mat_re, mat_im, eye):
    def diagonal(values, axis):
        return jnp.sum(jnp.where(eye, values, 0.0), axis=axis, keepdims=True)

    def reciprocal(axis):
        diag_re, diag_im = diagonal(mat_re, axis), diagonal(mat_im, axis)
        magnitude = diag_re * diag_re + diag_im * diag_im
        return diag_re / magnitude, -diag_im / magnitude

    col_re, col_im = reciprocal(1)
    row_re, row_im = reciprocal(0)
    outer_re = col_re * row_re - col_im * row_im
    outer_im = col_re * row_im + col_im * row_re
    first_re = jnp.where(eye, 2.0 * row_re, 0.0) - (outer_re * mat_re - outer_im * mat_im)
    first_im = jnp.where(eye, 2.0 * row_im, 0.0) - (outer_re * mat_im + outer_im * mat_re)
    first = (first_re, first_im)
    applied = cproduct(left_form((mat_re, mat_im)), right_form(first))
    second = cproduct(left_form(first), right_form(applied))
    return 2.0 * first_re - second[0], 2.0 * first_im - second[1]


def green_kernel(spacing, map_ref, ham_ref, hop_ref, self_ref, screened_ref, out_ref):
    order = ham_ref.shape[3]
    rows = lax.broadcasted_iota(jnp.int32, (order, order), 0)
    cols = lax.broadcasted_iota(jnp.int32, (order, order), 1)
    eye = rows == cols
    index = jnp.full((order, order), map_ref[0], jnp.int32).astype(jnp.float32)
    energy = energy_floor + spacing * index

    def put(block, row, values):
        start = block * order * field_rows + row
        out_ref[pl.ds(start, order, stride=field_rows), :] = values

    def shifted(block):
        raw_re, raw_im = ham_ref[0, block, 0], ham_ref[0, block, 1]
        herm_re = 0.5 * (raw_re + raw_re.T)
        herm_im = 0.5 * (raw_im - raw_im.T)
        return (
            jnp.where(eye, energy, 0.0) - herm_re - self_ref[0, 0, 0, block],
            jnp.where(eye, broadening, 0.0) - herm_im - self_ref[0, 0, 1, block],
        )

    for block in range(2):
        put(block, 2, screened_ref[0, 0, 0, block])
        put(block, 3, screened_ref[0, 0, 1, block])
        put(block, 4, index)
    hop = (hop_ref[0, 0], hop_ref[0, 1])
    adjoint = (hop[0].T, -hop[1].T)
    hop_right = right_form(hop)
    local = approx_inverse(*shifted(0), eye)
    incoming = cproduct(left_form(adjoint), right_form(local))
    outgoing = cproduct(left_form(local), hop_right)
    coupled = cproduct(left_form(incoming), hop_right)
    last = shifted(1)
    green = approx_inverse(last[0] - coupled[0], last[1] - coupled[1], eye)
    middle = cproduct(left_form(outgoing), right_form(green))
    middle = cproduct(left_form(middle), right_form(incoming))
    full = ((local[0] + middle[0], local[1] + middle[1]), green)
    for block in range(2):
        put(block, 0, -(full[block][1] + full[block][1].T))
        put(block, 1, full[block][0] - full[block][0].T)


def received(ref, row, scale=None):
    slots = ref.shape[0] // (2 * field_rows)

    def part(moment, n):
        start = moment * field_rows + row + n
        values = ref[pl.ds(start, slots, stride=2 * field_rows), :]
        return values if scale is None else scale * values

    return jnp.concatenate(
        [jnp.concatenate([part(0, n), part(1, n)], axis=1) for n in range(2)], axis=0
    )


def sigma_kernel(
    spacing, recv_ref, wave_ref, wave_t_ref, send_ref, fwd_ref, hat_ref, occ_ref
):
    slots, order = occ_ref.shape
    length = 2 * slots
    index = recv_ref[pl.ds(4, slots, stride=2 * field_rows), :]
    occupied = occupation(energy_floor + spacing * index)
    occ_ref[...] = occupied
    grid = lax.broadcasted_iota(jnp.int32, index.shape, 1).astype(jnp.float32)
    chosen = jnp.where(index == grid, 1.0, 0.0).astype(jnp.bfloat16)
    contract = (((1,), (1,)), ((), ()))
    forward, inverse = [], []
    for n in range(2):
        wave = [
            lax.dot_general(
                wave_ref[n, part], chosen, contract, preferred_element_type=jnp.float32
            ).astype(jnp.bfloat16)
            for part in range(2)
        ]
        forward.append(
            jnp.concatenate(
                [
                    jnp.concatenate([wave[0], -wave[1]], axis=1),
                    jnp.concatenate([wave[1], wave[0]], axis=1),
                ],
                axis=0,
            )
        )
        fwd_ref[n] = forward[n]
        turned = [dot(chosen, wave_t_ref[n, part]).astype(jnp.bfloat16) for part in range(2)]
        inverse.append(
            jnp.concatenate(
                [
                    jnp.concatenate([turned[0], turned[1]], axis=1),
                    jnp.concatenate([-turned[1], turned[0]], axis=1),
                ],
                axis=0,
            )
        )
    lesser = dot3(forward, halves(received(recv_ref, 0, occupied)))
    inter = dot3(forward, halves(received(recv_ref, 2)))
    hat_ref[...] = lesser

    def parts(hat, moment):
        return (
            hat[:length, moment * order : (moment + 1) * order],
            hat[length:, moment * order : (moment + 1) * order],
        )

    columns = []
    for moment in range(2):
        sum_re = sum_im = 0.0
        for transfer in range(2):
            left_re, left_im = parts(lesser, (moment - transfer) % 2)
            right_re, right_im = parts(inter, transfer)
            sum_re += left_re * right_re - left_im * right_im
            sum_im += left_re * right_im + left_im * right_re
        columns.append(jnp.concatenate([sum_re, sum_im], axis=0))
    result = dot3(inverse, halves(jnp.concatenate(columns, axis=1))) * (-spacing / length)
    for moment in range(2):
        for part in range(2):
            send_ref[pl.ds(moment * 2 + part, slots, stride=4), :] = result[
                part * slots : (part + 1) * slots, moment * order : (moment + 1) * order
            ]


def polar_kernel(
    spacing, mom_ref, recv_ref, occ_ref, fwd_ref, back_ref, hat_ref, keep_ref, give_ref, pol_ref
):
    slots, order = occ_ref.shape
    length = 2 * slots
    forward = (fwd_ref[0], fwd_ref[1])
    greater = dot3(forward, halves(received(recv_ref, 0, 1.0 - occ_ref[...])))

    def parts(hat, moment):
        return (
            hat[:length, moment * order : (moment + 1) * order],
            hat[length:, moment * order : (moment + 1) * order],
        )

    columns = []
    for transfer in range(2):
        sum_re = sum_im = 0.0
        for moment in range(2):
            left_re, left_im = parts(greater, moment)
            right_re, right_im = parts(hat_ref, (moment - transfer) % 2)
            sum_re += left_re * right_re + left_im * right_im
            sum_im += left_im * right_re - left_re * right_im
        columns.append(jnp.concatenate([sum_re, sum_im], axis=0))
    back = (back_ref[0], back_ref[1])
    result = dot3(back, halves(jnp.concatenate(columns, axis=1))) * (spacing / length)
    for transfer in range(2):
        chosen = result[:, transfer * order : (transfer + 1) * order]
        pol_ref[transfer, 0] = chosen[slots:]
        pol_ref[transfer, 1] = -chosen[:slots]
    keep_ref[...] = pol_ref[mom_ref[0]]
    give_ref[...] = pol_ref[1 - mom_ref[0]]


def finish_kernel(mom_ref, recv_ref, keep_ref, other_ref, sigma_ref, polar_ref):
    blocks, order = sigma_ref.shape[3], sigma_ref.shape[4]
    for part in range(2):
        for block in range(blocks):
            start = block * order * 2 + part
            sigma_ref[0, 0, part, block] = recv_ref[pl.ds(start, order, stride=2), :]
    first = mom_ref[0] == 0
    polar_ref[0, :, :, :order] = jnp.where(first, keep_ref[...], other_ref[...])
    polar_ref[0, :, :, order:] = jnp.where(first, other_ref[...], keep_ref[...])


def call(kernel, outs, scalars, name, scratch=()):
    vmem = pl.BlockSpec(memory_space=pltpu.VMEM)
    smem = pl.BlockSpec(memory_space=pltpu.SMEM)

    def run(*operands):
        return pl.pallas_call(
            kernel,
            out_shape=outs,
            in_specs=[smem] * scalars + [vmem] * (len(operands) - scalars),
            out_specs=jax.tree.map(lambda _: vmem, outs),
            scratch_shapes=list(scratch),
            name=name,
        )(*operands)

    return run


def exchange(chunks):
    return lax.all_to_all(chunks, ("energy", "mom"), split_axis=0, concat_axis=0, tiled=True)


def split_table(table):
    high = table.astype(np.float32).astype(jnp.bfloat16)
    low = (table - high.astype(np.float64)).astype(np.float32).astype(jnp.bfloat16)
    return np.stack([high, low])


def on_device(hamiltonian, hopping, self_energy, screened, energy_map):
    slots = lax.axis_size("energy")
    spacing = energy_span / slots
    length = 2 * slots
    order = hamiltonian.shape[-1]
    angle = (np.arange(length)[:, None] * np.arange(slots)[None, :] % length) * (
        2.0 * math.pi / length
    )
    wave = np.stack([np.cos(angle), -np.sin(angle)])
    wave_t = np.swapaxes(wave, 1, 2)
    back = np.block([[wave_t[0], wave_t[1]], [-wave_t[1], wave_t[0]]])
    wave, wave_t, back = (jnp.asarray(split_table(t)) for t in (wave, wave_t, back))

    def f32(*shape):
        return jax.ShapeDtypeStruct(shape, jnp.float32)

    def b16(*shape):
        return jax.ShapeDtypeStruct(shape, jnp.bfloat16)

    moment = lax.axis_index("mom").astype(jnp.int32).reshape(1)
    targets = 2 * slots
    fields = call(
        lambda *refs: green_kernel(spacing, *refs), f32(targets * field_rows, order), 1, "green"
    )(energy_map, hamiltonian, hopping, self_energy, screened)
    own = exchange(fields.reshape(targets, 1, field_rows * order)).reshape(fields.shape)
    send, forward, lesser_hat, occupied = call(
        lambda *refs: sigma_kernel(spacing, *refs),
        (
            f32(2 * targets, order),
            b16(2, 2 * length, 2 * slots),
            f32(2 * length, 2 * order),
            f32(slots, order),
        ),
        0,
        "sigma",
    )(own, wave, wave_t)
    returned = exchange(send.reshape(targets, 2, order)).reshape(send.shape)
    keep, give = call(
        lambda *refs: polar_kernel(spacing, *refs),
        (f32(2, slots, order), f32(2, slots, order)),
        1,
        "polar",
        [pltpu.VMEM((2, 2, slots, order), jnp.float32)],
    )(moment, own, occupied, forward, back, lesser_hat)
    other = from_partner(give, "mom")
    new_sigma, polar = call(
        finish_kernel, (f32(*screened.shape), f32(1, 2, slots, 2 * order)), 1, "finish"
    )(moment, returned, keep, other)
    return (new_sigma, polar)


def solution(mesh):
    return jax.shard_map(
        on_device,
        mesh=mesh,
        in_specs=(
            P("mom", None, None, None, None),
            P("mom", None, None, None),
            P("mom", "energy", None, None, None, None),
            P("mom", "energy", None, None, None, None),
            P("energy"),
        ),
        out_specs=(P("mom", "energy", None, None, None, None), P("mom", None, None, "energy")),
        check_vma=False,
    )
```

time: 105 us -> 72 us (0.69)
  blocking collectives: 0 us -> 38.6 us
  waiting for transfers between devices: 46.3 us -> 10.6 us
  starting transfers between devices: 36.4 us -> 7.53 us
  Pallas kernels: 18.1 us -> 13 us
  local copies, waits for them, and re-layouts: 2.12 us -> 0.7 us
    all_to_all x0 -> x1, blocking collectives: none -> 38.6 us  [exchange(): lax.all_to_all(chunks, ('energy', 'mom'), split_axis=0, concat_axis=0, ti...]
    all_to_all x3 -> x1, starting transfers between devices: 35.5 us -> 6.14 us  [exchange(): lax.all_to_all(chunks, ('energy', 'mom'), split_axis=0, concat_axis=0, ti...]
    all_to_all x3 -> x1, waiting for transfers between devices: 28.6 us -> 6.65 us  [exchange(): lax.all_to_all(chunks, ('energy', 'mom'), split_axis=0, concat_axis=0, ti...]
    ppermute x2 -> x1, waiting for transfers between devices: 17.7 us -> 3.94 us  [from_partner(): lax.ppermute(array, axis, [(i, i ^ 1) for i in range(lax.axis_size(axis))])]
    pallas_call x6 -> x4, Pallas kernels: 18.1 us -> 13 us  [run(): pl.pallas_call(kernel, out_shape=outs, in_specs=[smem] * scalars + [vmem]...]
    unnamed x10 -> x4, local copies, waits for them, and re-layouts: 2.12 us -> 0.7 us
  transfers between devices with their start and end apart: 5 -> 2, of which waited for: 5 -> 2; matrix products, arithmetic and copies ran while one was open for 0% -> 0% of each run, Pallas kernels for 10% -> 5%
where the time goes in v2:
time: 72 us; the launch traced here: 71.7 us
  blocking collectives  38.6 us (54%)
  Pallas kernels  13 us (18%)
  waiting for transfers between devices  10.6 us (15%)
  starting transfers between devices  7.53 us (10%)
  between operations  1.3 us (2%)
    all_to_all x1, blocking collectives, exchange(): lax.all_to_all(chunks, ('energy', 'mom'), split_axis=0, concat_axis=0, ti...  38.6 us
    pallas_call x4, Pallas kernels, run(): pl.pallas_call(kernel, out_shape=outs, in_specs=[smem] * scalars + [vmem]...  13 us
    all_to_all x1, waiting for transfers between devices, exchange(): lax.all_to_all(chunks, ('energy', 'mom'), split_axis=0, concat_axis=0, ti...  6.65 us
    all_to_all x1, starting transfers between devices, exchange(): lax.all_to_all(chunks, ('energy', 'mom'), split_axis=0, concat_axis=0, ti...  6.14 us
    ppermute x1, waiting for transfers between devices, from_partner(): lax.ppermute(array, axis, [(i, i ^ 1) for i in range(lax.axis_size(axis))])  3.94 us
  transfers between devices with their start and end apart: 2, of which 2 were waited for; matrix products, arithmetic and copies ran while one was open for 0% of the time, Pallas kernels for 5%

profile of v2, /device:TPU:1, one launch (start us, length us, event | category | flops | bytes accessed | tf_op | source)
XLA Modules:
  0.0 71.7 jit_solution(12025049089144765397)
XLA Ops:
  1.3 4.2 %green.1 = f32[1280,128]{1,0:T(8,128)} custom-call(s32[1]{0:T(128)S(6)} %copy.11.refs_0_, f32[1,2,2,128,128]{4,3,2,1,0:T(8,128)} %refs_1_.2, f32[1,2,128,128]{3,2,1,0:T(8,128)} %refs_2_.2, f32[1,1,2,2,128,128]{5,4,3,2,1,0:T(8,128)} %refs_3_.1, f32[1,1,2,2,128,128]{5,4,3,2,1,0:T(8,128)} %refs_4_.2), custom_call_target="tpu_custom_call" | custom-call | tf_op jit(solution)/shard_map/green/pallas_call | solution.py:253
  5.5 38.6 %all_to_all.10 = f32[256,1,640]{2,1,0:T(1,128)} all-to-all(f32[256,1,640]{2,1,0:T(1,128)} %bitcast.7), channel_id=1, replica_groups=mesh['energy'=128,'mom'=2] {'energy','mom'}, dimensions={0} | all-to-all | bytes 1310720 | tf_op jit(solution)/shard_map/all_to_all | solution.py:266
  44.1 3.5 %sigma.1 = (f32[512,128]{1,0:T(8,128)}, bf16[2,512,256]{2,1,0:T(8,128)(2,1)}, f32[512,256]{1,0:T(8,128)}, f32[128,128]{1,0:T(8,128)}) custom-call(f32[1280,128]{1,0:T(8,128)} %bitcast.5, bf16[2,2,256,128]{3,2,1,0:T(8,128)(2,1)} %constant.10.clone.refs_1_, bf16[2,2,128,256]{3,2,1,0:T(8,128)(2,1)} %constant.11.clone.refs_2_), custom_call_target="tpu_custom_call" | custom-call | tf_op jit(solution)/shard_map/sigma/pallas_call | solution.py:253
  47.6 6.1 %all-to-all-start.1 = ((f32[256,2,128]{2,1,0:T(2,128)}), f32[256,2,128]{2,1,0:T(2,128)S(1)}, u32[]{:S(2)}, u32[]{:S(2)}) async-start(f32[256,2,128]{2,1,0:T(2,128)} %bitcast.9), calls=%async_computation.1 | async-start | bytes 524288 | tf_op jit(solution)/shard_map/all_to_all | solution.py:266
  53.7 3.4 %polar.1 = (f32[2,128,128]{2,1,0:T(8,128)}, f32[2,128,128]{2,1,0:T(8,128)}) custom-call(s32[1]{0:T(128)} %bitcast.refs_0_.mom_ref, f32[1280,128]{1,0:T(8,128)} %bitcast.6, f32[128,128]{1,0:T(8,128)} %get-tuple-element.9.refs_2_, bf16[2,512,256]{2,1,0:T(8,128)(2,1)} %get-tuple-element.10.refs_3_, bf16[2,256,512]{2,1,0:T(8,128)(2,1)} %constant.12.clone.refs_4_, ...), custom_call_target="tpu_custom_call" | custom-call | tf_op jit(solution)/shard_map/polar/pallas_call | solution.py:253
  57.2 1.4 %collective-permute-start = (f32[2,128,128]{2,1,0:T(8,128)}, f32[2,128,128]{2,1,0:T(8,128)S(1)}, u32[]{:S(2)}, u32[]{:S(2)}) collective-permute-start(f32[2,128,128]{2,1,0:T(8,128)} %get-tuple-element.13), channel_id=1, source_target_pairs={{0,1},{1,0},{2,3},{3,2},{4,5},{5,4},{6,7},{7,6},{8,9},{9,8},{10,11... | collective-permute-start | bytes 393224 | tf_op jit(solution)/shard_map/ppermute | solution.py:21
  58.6 3.9 %collective-permute-done.other_ref = f32[2,128,128]{2,1,0:T(8,128)S(1)} collective-permute-done((f32[2,128,128]{2,1,0:T(8,128)}, f32[2,128,128]{2,1,0:T(8,128)S(1)}, u32[]{:S(2)}, u32[]{:S(2)}) %collective-permute-start) | collective-permute-done | bytes 131104 | tf_op jit(solution)/shard_map/ppermute | solution.py:21
  62.5 0.0 copy-start.1
  62.5 6.7 %all-to-all-done.1 = f32[256,2,128]{2,1,0:T(2,128)S(1)} async-done(((f32[256,2,128]{2,1,0:T(2,128)}), f32[256,2,128]{2,1,0:T(2,128)S(1)}, u32[]{:S(2)}, u32[]{:S(2)}) %all-to-all-start.1) | async-done | bytes 262176 | tf_op jit(solution)/shard_map/all_to_all | solution.py:266
  69.2 0.0 copy-start
  69.2 0.0 copy-done.1
  69.2 0.7 copy-done
  69.9 1.9 %finish.1 = (f32[1,1,2,2,128,128]{5,4,3,2,1,0:T(8,128)}, f32[1,2,128,256]{3,2,1,0:T(8,128)}) custom-call(s32[1]{0:T(128)} %bitcast.refs_0_.mom_ref, f32[512,128]{1,0:T(8,128)} %bitcast.8, f32[2,128,128]{2,1,0:T(8,128)} %get-tuple-element.12.keep_ref, f32[2,128,128]{2,1,0:T(8,128)} %copy-done.1), custom_call_target="tpu_custom_call" | custom-call | tf_op jit(solution)/shard_map/finish/pallas_call | solution.py:253
Async XLA Ops:
  47.6 21.6 %all-to-all-start.1 = ((f32[256,2,128]{2,1,0:T(2,128)}), f32[256,2,128]{2,1,0:T(2,128)S(1)}, u32[]{:S(2)}, u32[]{:S(2)}) async-start(f32[256,2,128]{2,1,0:T(2,128)} %bitcast.9), calls=%async_computation.1 | async-start | bytes 524288 | tf_op jit(solution)/shard_map/all_to_all | solution.py:266
  57.2 5.3 %collective-permute-start = (f32[2,128,128]{2,1,0:T(8,128)}, f32[2,128,128]{2,1,0:T(8,128)S(1)}, u32[]{:S(2)}, u32[]{:S(2)}) collective-permute-start(f32[2,128,128]{2,1,0:T(8,128)} %get-tuple-element.13), channel_id=1, source_target_pairs={{0,1},{1,0},{2,3},{3,2},{4,5},{5,4},{6,7},{7,6},{8,9},{9,8},{10,11... | collective-permute-start | bytes 393224 | tf_op jit(solution)/shard_map/ppermute | solution.py:21
  62.5 6.7 %copy-start.1 = (f32[2,128,128]{2,1,0:T(8,128)}, f32[2,128,128]{2,1,0:T(8,128)S(1)}, u32[]{:S(2)}) copy-start(f32[2,128,128]{2,1,0:T(8,128)S(1)} %collective-permute-done.other_ref) | copy-start | bytes 393220
  69.2 0.7 copy-start

commit v3 on v2

--- a/solution.py
+++ b/solution.py
@@ -14,7 +14,7 @@
 chemical = 0.0
 thermal = 0.25
 
-field_rows = 5
+field_rows = 4
 
 
 def from_partner(array, axis):
@@ -104,7 +104,6 @@
     for block in range(2):
         put(block, 2, screened_ref[0, 0, 0, block])
         put(block, 3, screened_ref[0, 0, 1, block])
-        put(block, 4, index)
     hop = (hop_ref[0, 0], hop_ref[0, 1])
     adjoint = (hop[0].T, -hop[1].T)
     hop_right = right_form(hop)
@@ -119,28 +118,48 @@
     full = ((local[0] + middle[0], local[1] + middle[1]), green)
     for block in range(2):
         put(block, 0, -(full[block][1] + full[block][1].T))
-        put(block, 1, full[block][0] - full[block][0].T)
-
-
-def received(ref, row, scale=None):
+        put(block, 1, jnp.where(eye, index, full[block][0] - full[block][0].T))
+
+
+def rows_of(ref, moment, row):
     slots = ref.shape[0] // (2 * field_rows)
-
-    def part(moment, n):
-        start = moment * field_rows + row + n
-        values = ref[pl.ds(start, slots, stride=2 * field_rows), :]
-        return values if scale is None else scale * values
-
+    return ref[pl.ds(moment * field_rows + row, slots, stride=2 * field_rows), :]
+
+
+def on_diagonal(column_ref, shape):
+    return lax.broadcasted_iota(jnp.int32, shape, 1) == column_ref[0]
+
+
+def spectrum(ref, diagonal, scale):
+    real = [scale * rows_of(ref, moment, 0) for moment in range(2)]
+    imag = [
+        jnp.where(diagonal, 0.0, scale * rows_of(ref, moment, 1)) for moment in range(2)
+    ]
     return jnp.concatenate(
-        [jnp.concatenate([part(0, n), part(1, n)], axis=1) for n in range(2)], axis=0
+        [jnp.concatenate(real, axis=1), jnp.concatenate(imag, axis=1)], axis=0
+    )
+
+
+def interaction(ref):
+    return jnp.concatenate(
+        [
+            jnp.concatenate([rows_of(ref, moment, row) for moment in range(2)], axis=1)
+            for row in (2, 3)
+        ],
+        axis=0,
     )
 
 
 def sigma_kernel(
-    spacing, recv_ref, wave_ref, wave_t_ref, send_ref, fwd_ref, hat_ref, occ_ref
+    spacing, column_ref, recv_ref, wave_ref, wave_t_ref, send_ref, fwd_ref, hat_ref, occ_ref
 ):
     slots, order = occ_ref.shape
     length = 2 * slots
-    index = recv_ref[pl.ds(4, slots, stride=2 * field_rows), :]
+    diagonal = on_diagonal(column_ref, occ_ref.shape)
+    index = jnp.sum(
+        jnp.where(diagonal, rows_of(recv_ref, 0, 1), 0.0), axis=1, keepdims=True
+    )
+    index = jnp.broadcast_to(index, occ_ref.shape)
     occupied = occupation(energy_floor + spacing * index)
     occ_ref[...] = occupied
     grid = lax.broadcasted_iota(jnp.int32, index.shape, 1).astype(jnp.float32)
@@ -174,8 +193,8 @@
                 axis=0,
             )
         )
-    lesser = dot3(forward, halves(received(recv_ref, 0, occupied)))
-    inter = dot3(forward, halves(received(recv_ref, 2)))
+    lesser = dot3(forward, halves(spectrum(recv_ref, diagonal, occupied)))
+    inter = dot3(forward, halves(interaction(recv_ref)))
     hat_ref[...] = lesser
 
     def parts(hat, moment):
@@ -202,12 +221,23 @@
 
 
 def polar_kernel(
-    spacing, mom_ref, recv_ref, occ_ref, fwd_ref, back_ref, hat_ref, keep_ref, give_ref, pol_ref
+    spacing,
+    mom_ref,
+    column_ref,
+    recv_ref,
+    occ_ref,
+    fwd_ref,
+    back_ref,
+    hat_ref,
+    keep_ref,
+    give_ref,
+    pol_ref,
 ):
     slots, order = occ_ref.shape
     length = 2 * slots
     forward = (fwd_ref[0], fwd_ref[1])
-    greater = dot3(forward, halves(received(recv_ref, 0, 1.0 - occ_ref[...])))
+    diagonal = on_diagonal(column_ref, occ_ref.shape)
+    greater = dot3(forward, halves(spectrum(recv_ref, diagonal, 1.0 - occ_ref[...])))
 
     def parts(hat, moment):
         return (
@@ -234,15 +264,11 @@
     give_ref[...] = pol_ref[1 - mom_ref[0]]
 
 
-def finish_kernel(mom_ref, recv_ref, keep_ref, other_ref, sigma_ref, polar_ref):
-    blocks, order = sigma_ref.shape[3], sigma_ref.shape[4]
-    for part in range(2):
-        for block in range(blocks):
-            start = block * order * 2 + part
-            sigma_ref[0, 0, part, block] = recv_ref[pl.ds(start, order, stride=2), :]
+def join_kernel(mom_ref, keep_ref, other_ref, out_ref):
+    order = keep_ref.shape[2]
     first = mom_ref[0] == 0
-    polar_ref[0, :, :, :order] = jnp.where(first, keep_ref[...], other_ref[...])
-    polar_ref[0, :, :, order:] = jnp.where(first, other_ref[...], keep_ref[...])
+    out_ref[0, :, :, :order] = jnp.where(first, keep_ref[...], other_ref[...])
+    out_ref[0, :, :, order:] = jnp.where(first, other_ref[...], keep_ref[...])
 
 
 def call(kernel, outs, scalars, name, scratch=()):
@@ -293,10 +319,11 @@
 
     moment = lax.axis_index("mom").astype(jnp.int32).reshape(1)
     targets = 2 * slots
+    column = lax.axis_index(("energy", "mom")).astype(jnp.int32).reshape(1) % order
     fields = call(
         lambda *refs: green_kernel(spacing, *refs), f32(targets * field_rows, order), 1, "green"
     )(energy_map, hamiltonian, hopping, self_energy, screened)
-    own = exchange(fields.reshape(targets, 1, field_rows * order)).reshape(fields.shape)
+    own = exchange(fields.reshape(targets, field_rows, order)).reshape(fields.shape)
     send, forward, lesser_hat, occupied = call(
         lambda *refs: sigma_kernel(spacing, *refs),
         (
@@ -305,21 +332,20 @@
             f32(2 * length, 2 * order),
             f32(slots, order),
         ),
-        0,
+        1,
         "sigma",
-    )(own, wave, wave_t)
-    returned = exchange(send.reshape(targets, 2, order)).reshape(send.shape)
+    )(column, own, wave, wave_t)
+    returned = exchange(send.reshape(targets, 2, order))
     keep, give = call(
         lambda *refs: polar_kernel(spacing, *refs),
         (f32(2, slots, order), f32(2, slots, order)),
-        1,
+        2,
         "polar",
         [pltpu.VMEM((2, 2, slots, order), jnp.float32)],
-    )(moment, own, occupied, forward, back, lesser_hat)
+    )(moment, column, own, occupied, forward, back, lesser_hat)
     other = from_partner(give, "mom")
-    new_sigma, polar = call(
-        finish_kernel, (f32(*screened.shape), f32(1, 2, slots, 2 * order)), 1, "finish"
-    )(moment, returned, keep, other)
+    polar = call(join_kernel, f32(1, 2, slots, 2 * order), 1, "join")(moment, keep, other)
+    new_sigma = jnp.swapaxes(returned, 0, 1).reshape(screened.shape)
     return (new_sigma, polar)
 
 

time: 72 us -> 68.3 us (0.949)
  blocking collectives: 38.6 us -> 0 us
  waiting for transfers between devices: 10.6 us -> 28.8 us
  starting transfers between devices: 7.53 us -> 22.9 us
  local copies, waits for them, and re-layouts: 0.7 us -> 2.17 us
    all_to_all x1 -> x0, blocking collectives: 38.6 us -> none  [exchange(): lax.all_to_all(chunks, ('energy', 'mom'), split_axis=0, concat_axis=0, ti...]
    all_to_all x1 -> x2, waiting for transfers between devices: 6.65 us -> 24.9 us  [exchange(): lax.all_to_all(chunks, ('energy', 'mom'), split_axis=0, concat_axis=0, ti...]
    all_to_all x1 -> x2, starting transfers between devices: 6.14 us -> 21.5 us  [exchange(): lax.all_to_all(chunks, ('energy', 'mom'), split_axis=0, concat_axis=0, ti...]
    unnamed x4, local copies, waits for them, and re-layouts: 0.7 us -> 1.45 us
    transpose x0 -> x1, local copies, waits for them, and re-layouts: none -> 0.72 us  [on_device(): new_sigma = jnp.swapaxes(returned, 0, 1).reshape(screened.shape)]
  transfers between devices with their start and end apart: 2 -> 3, of which waited for: 2 -> 3; matrix products, arithmetic and copies ran while one was open for 0% -> 0% of each run, Pallas kernels for 5% -> 8%
where the time goes in v3:
time: 68.3 us; the launch traced here: 68 us
  waiting for transfers between devices  28.8 us (42%)
  starting transfers between devices  22.9 us (34%)
  Pallas kernels  12.8 us (19%)
  local copies, waits for them, and re-layouts  2.17 us (3%)
  between operations  1.31 us (2%)
    all_to_all x2, waiting for transfers between devices, exchange(): lax.all_to_all(chunks, ('energy', 'mom'), split_axis=0, concat_axis=0, ti...  24.9 us
    all_to_all x2, starting transfers between devices, exchange(): lax.all_to_all(chunks, ('energy', 'mom'), split_axis=0, concat_axis=0, ti...  21.5 us
    pallas_call x4, Pallas kernels, run(): pl.pallas_call(kernel, out_shape=outs, in_specs=[smem] * scalars + [vmem]...  12.8 us
    ppermute x1, waiting for transfers between devices, from_partner(): lax.ppermute(array, axis, [(i, i ^ 1) for i in range(lax.axis_size(axis))])  3.86 us
    unnamed x4, local copies, waits for them, and re-layouts  1.45 us
    ppermute x1, starting transfers between devices, from_partner(): lax.ppermute(array, axis, [(i, i ^ 1) for i in range(lax.axis_size(axis))])  1.44 us
  transfers between devices with their start and end apart: 3, of which 3 were waited for; matrix products, arithmetic and copies ran while one was open for 0% of the time, Pallas kernels for 8%

profile of v3, /device:TPU:1, one launch (start us, length us, event | category | flops | bytes accessed | tf_op | source)
XLA Modules:
  0.0 68.0 jit_solution(8858006729461768272)
XLA Ops:
  1.3 4.2 %green.1 = f32[1024,128]{1,0:T(8,128)} custom-call(s32[1]{0:T(128)S(6)} %copy.11.refs_0_, f32[1,2,2,128,128]{4,3,2,1,0:T(8,128)} %refs_1_.1, f32[1,2,128,128]{3,2,1,0:T(8,128)} %refs_2_.2, f32[1,1,2,2,128,128]{5,4,3,2,1,0:T(8,128)} %refs_3_.2, f32[1,1,2,2,128,128]{5,4,3,2,1,0:T(8,128)} %refs_4_.1), custom_call_target="tpu_custom_call" | custom-call | tf_op jit(solution)/shard_map/green/pallas_call | solution.py:279
  5.5 15.7 %all-to-all-start = ((f32[256,4,128]{2,1,0:T(4,128)}), f32[256,4,128]{2,1,0:T(4,128)S(1)}, u32[]{:S(2)}, u32[]{:S(2)}) async-start(f32[256,4,128]{2,1,0:T(4,128)} %bitcast.9), calls=%async_computation | async-start | bytes 1048576 | tf_op jit(solution)/shard_map/all_to_all | solution.py:292
  21.2 20.4 %all-to-all-done = f32[256,4,128]{2,1,0:T(4,128)S(1)} async-done(((f32[256,4,128]{2,1,0:T(4,128)}), f32[256,4,128]{2,1,0:T(4,128)S(1)}, u32[]{:S(2)}, u32[]{:S(2)}) %all-to-all-start) | async-done | bytes 524320 | tf_op jit(solution)/shard_map/all_to_all | solution.py:292
  41.6 0.0 copy-start
  41.6 0.8 %copy-done = f32[256,4,128]{2,1,0:T(4,128)} copy-done((f32[256,4,128]{2,1,0:T(4,128)}, f32[256,4,128]{2,1,0:T(4,128)S(1)}, u32[]{:S(2)}) %copy-start) | copy-done | bytes 524312
  42.4 3.5 %sigma.1 = (f32[512,128]{1,0:T(8,128)}, bf16[2,512,256]{2,1,0:T(8,128)(2,1)}, f32[512,256]{1,0:T(8,128)}, f32[128,128]{1,0:T(8,128)}) custom-call(s32[1]{0:T(128)S(6)} %select_n.7.refs_0_.refs_1_, f32[1024,128]{1,0:T(8,128)} %bitcast.7, bf16[2,2,256,128]{3,2,1,0:T(8,128)(2,1)} %constant.35.clone.refs_2_, bf16[2,2,128,256]{3,2,1,0:T(8,128)(2,1)} %constant.36.clone.refs_3_), custom_call_target="tpu_custom_call" | custom-call | tf_op jit(solution)/shard_map/sigma/pallas_call | solution.py:279
  45.9 5.8 %all-to-all-start.1 = ((f32[256,2,128]{2,1,0:T(2,128)}), f32[256,2,128]{2,1,0:T(2,128)S(1)}, u32[]{:S(2)}, u32[]{:S(2)}) async-start(f32[256,2,128]{2,1,0:T(2,128)} %bitcast.11), calls=%async_computation.1 | async-start | bytes 524288 | tf_op jit(solution)/shard_map/all_to_all | solution.py:292
  51.7 3.4 %polar.1 = (f32[2,128,128]{2,1,0:T(8,128)}, f32[2,128,128]{2,1,0:T(8,128)}) custom-call(s32[1]{0:T(128)} %bitcast.6.refs_0_.mom_ref, s32[1]{0:T(128)S(6)} %select_n.7.refs_0_.refs_1_, f32[1024,128]{1,0:T(8,128)} %bitcast.8, f32[128,128]{1,0:T(8,128)} %get-tuple-element.9.refs_3_, bf16[2,512,256]{2,1,0:T(8,128)(2,1)} %get-tuple-element.10.refs_4_, ...), custom_call_target="tpu_custom_call" | custom-call | tf_op jit(solution)/shard_map/polar/pallas_call | solution.py:279
  55.1 1.4 %collective-permute-start = (f32[2,128,128]{2,1,0:T(8,128)}, f32[2,128,128]{2,1,0:T(8,128)S(1)}, u32[]{:S(2)}, u32[]{:S(2)}) collective-permute-start(f32[2,128,128]{2,1,0:T(8,128)} %get-tuple-element.13), channel_id=1, source_target_pairs={{0,1},{1,0},{2,3},{3,2},{4,5},{5,4},{6,7},{7,6},{8,9},{9,8},{10,11... | collective-permute-start | bytes 393224 | tf_op jit(solution)/shard_map/ppermute | solution.py:21
  56.6 3.9 %collective-permute-done.other_ref = f32[2,128,128]{2,1,0:T(8,128)S(1)} collective-permute-done((f32[2,128,128]{2,1,0:T(8,128)}, f32[2,128,128]{2,1,0:T(8,128)S(1)}, u32[]{:S(2)}, u32[]{:S(2)}) %collective-permute-start) | collective-permute-done | bytes 131104 | tf_op jit(solution)/shard_map/ppermute | solution.py:21
  60.5 0.0 copy-start.1
  60.5 0.6 copy-done.1
  61.1 1.7 %join.1 = f32[1,2,128,256]{3,2,1,0:T(8,128)} custom-call(s32[1]{0:T(128)} %bitcast.6.refs_0_.mom_ref, f32[2,128,128]{2,1,0:T(8,128)} %get-tuple-element.12.keep_ref, f32[2,128,128]{2,1,0:T(8,128)} %copy-done.1), custom_call_target="tpu_custom_call" | custom-call | tf_op jit(solution)/shard_map/join/pallas_call | solution.py:279
  62.8 4.5 %all-to-all-done.1 = f32[256,2,128]{2,1,0:T(2,128)S(1)} async-done(((f32[256,2,128]{2,1,0:T(2,128)}), f32[256,2,128]{2,1,0:T(2,128)S(1)}, u32[]{:S(2)}, u32[]{:S(2)}) %all-to-all-start.1) | async-done | bytes 262176 | tf_op jit(solution)/shard_map/all_to_all | solution.py:292
  67.3 0.7 %copy.10 = f32[2,256,128]{2,1,0:T(8,128)} copy(f32[2,256,128]{2,0,1:T(2,128)S(1)} %bitcast.10) | data formatting | bytes 524288 | tf_op jit(solution)/shard_map/transpose | solution.py:348
Async XLA Ops:
  5.5 36.1 %all-to-all-start = ((f32[256,4,128]{2,1,0:T(4,128)}), f32[256,4,128]{2,1,0:T(4,128)S(1)}, u32[]{:S(2)}, u32[]{:S(2)}) async-start(f32[256,4,128]{2,1,0:T(4,128)} %bitcast.9), calls=%async_computation | async-start | bytes 1048576 | tf_op jit(solution)/shard_map/all_to_all | solution.py:292
  41.6 0.8 %copy-start = (f32[256,4,128]{2,1,0:T(4,128)}, f32[256,4,128]{2,1,0:T(4,128)S(1)}, u32[]{:S(2)}) copy-start(f32[256,4,128]{2,1,0:T(4,128)S(1)} %all-to-all-done) | copy-start | bytes 1572868
  45.9 21.4 %all-to-all-start.1 = ((f32[256,2,128]{2,1,0:T(2,128)}), f32[256,2,128]{2,1,0:T(2,128)S(1)}, u32[]{:S(2)}, u32[]{:S(2)}) async-start(f32[256,2,128]{2,1,0:T(2,128)} %bitcast.11), calls=%async_computation.1 | async-start | bytes 524288 | tf_op jit(solution)/shard_map/all_to_all | solution.py:292
  55.1 5.3 %collective-permute-start = (f32[2,128,128]{2,1,0:T(8,128)}, f32[2,128,128]{2,1,0:T(8,128)S(1)}, u32[]{:S(2)}, u32[]{:S(2)}) collective-permute-start(f32[2,128,128]{2,1,0:T(8,128)} %get-tuple-element.13), channel_id=1, source_target_pairs={{0,1},{1,0},{2,3},{3,2},{4,5},{5,4},{6,7},{7,6},{8,9},{9,8},{10,11... | collective-permute-start | bytes 393224 | tf_op jit(solution)/shard_map/ppermute | solution.py:21
  60.5 0.6 copy-start.1

commit v4 on v3

--- a/solution.py
+++ b/solution.py
@@ -288,6 +288,10 @@
     return run
 
 
+def resident(array):
+    return pltpu.with_memory_space_constraint(array, pltpu.VMEM)
+
+
 def exchange(chunks):
     return lax.all_to_all(chunks, ("energy", "mom"), split_axis=0, concat_axis=0, tiled=True)
 
@@ -314,37 +318,47 @@
     def f32(*shape):
         return jax.ShapeDtypeStruct(shape, jnp.float32)
 
-    def b16(*shape):
-        return jax.ShapeDtypeStruct(shape, jnp.bfloat16)
-
     moment = lax.axis_index("mom").astype(jnp.int32).reshape(1)
+    def held(*shape, kind=jnp.float32):
+        return pltpu.VMEM(shape, kind)
+
     targets = 2 * slots
     column = lax.axis_index(("energy", "mom")).astype(jnp.int32).reshape(1) % order
     fields = call(
         lambda *refs: green_kernel(spacing, *refs), f32(targets * field_rows, order), 1, "green"
     )(energy_map, hamiltonian, hopping, self_energy, screened)
-    own = exchange(fields.reshape(targets, field_rows, order)).reshape(fields.shape)
+    own = resident(exchange(fields.reshape(targets, field_rows, order)).reshape(fields.shape))
     send, forward, lesser_hat, occupied = call(
         lambda *refs: sigma_kernel(spacing, *refs),
         (
             f32(2 * targets, order),
-            b16(2, 2 * length, 2 * slots),
-            f32(2 * length, 2 * order),
-            f32(slots, order),
+            held(2, 2 * length, 2 * slots, kind=jnp.bfloat16),
+            held(2 * length, 2 * order),
+            held(slots, order),
         ),
         1,
         "sigma",
-    )(column, own, wave, wave_t)
+    )(column, own, resident(wave), resident(wave_t))
     returned = exchange(send.reshape(targets, 2, order))
     keep, give = call(
         lambda *refs: polar_kernel(spacing, *refs),
-        (f32(2, slots, order), f32(2, slots, order)),
+        (held(2, slots, order), held(2, slots, order)),
         2,
         "polar",
         [pltpu.VMEM((2, 2, slots, order), jnp.float32)],
-    )(moment, column, own, occupied, forward, back, lesser_hat)
-    other = from_partner(give, "mom")
-    polar = call(join_kernel, f32(1, 2, slots, 2 * order), 1, "join")(moment, keep, other)
+    )(
+        moment,
+        column,
+        own,
+        resident(occupied),
+        resident(forward),
+        resident(back),
+        resident(lesser_hat),
+    )
+    other = resident(from_partner(give, "mom"))
+    polar = call(join_kernel, f32(1, 2, slots, 2 * order), 1, "join")(
+        moment, resident(keep), other
+    )
     new_sigma = jnp.swapaxes(returned, 0, 1).reshape(screened.shape)
     return (new_sigma, polar)
 

time: 68.3 us -> 66.4 us (0.972)
  Pallas kernels: 12.8 us -> 8.43 us
  waiting for transfers between devices: 28.8 us -> 32.6 us
  local copies, waits for them, and re-layouts: 2.17 us -> 0.73 us
    all_to_all x2, waiting for transfers between devices: 24.9 us -> 29.4 us  [exchange(): lax.all_to_all(chunks, ('energy', 'mom'), split_axis=0, concat_axis=0, ti...]
    pallas_call x4, Pallas kernels: 12.8 us -> 8.43 us  [run(): pl.pallas_call(kernel, out_shape=outs, in_specs=[smem] * scalars + [vmem]...]
    unnamed x4 -> x6, local copies, waits for them, and re-layouts: 1.45 us -> 0.01 us
    ppermute x1, waiting for transfers between devices: 3.86 us -> 3.15 us  [from_partner(): lax.ppermute(array, axis, [(i, i ^ 1) for i in range(lax.axis_size(axis))])]
  transfers between devices with their start and end apart: 3 -> 3, of which waited for: 3 -> 3; matrix products, arithmetic and copies ran while one was open for 0% -> 0% of each run, Pallas kernels for 8% -> 3%
where the time goes in v4:
time: 66.4 us; the launch traced here: 66.2 us
  waiting for transfers between devices  32.6 us (49%)
  starting transfers between devices  23.1 us (35%)
  Pallas kernels  8.43 us (13%)
  between operations  1.33 us (2%)
  local copies, waits for them, and re-layouts  0.73 us (1%)
    all_to_all x2, waiting for transfers between devices, exchange(): lax.all_to_all(chunks, ('energy', 'mom'), split_axis=0, concat_axis=0, ti...  29.4 us
    all_to_all x2, starting transfers between devices, exchange(): lax.all_to_all(chunks, ('energy', 'mom'), split_axis=0, concat_axis=0, ti...  21.6 us
    pallas_call x4, Pallas kernels, run(): pl.pallas_call(kernel, out_shape=outs, in_specs=[smem] * scalars + [vmem]...  8.43 us
    ppermute x1, waiting for transfers between devices, from_partner(): lax.ppermute(array, axis, [(i, i ^ 1) for i in range(lax.axis_size(axis))])  3.15 us
    ppermute x1, starting transfers between devices, from_partner(): lax.ppermute(array, axis, [(i, i ^ 1) for i in range(lax.axis_size(axis))])  1.53 us
  transfers between devices with their start and end apart: 3, of which 3 were waited for; matrix products, arithmetic and copies ran while one was open for 0% of the time, Pallas kernels for 3%

profile of v4, /device:TPU:1, one launch (start us, length us, event | category | flops | bytes accessed | tf_op | source)
XLA Modules:
  0.0 66.2 jit_solution(3084094636523819962)
XLA Ops:
  1.3 4.2 %green.1 = f32[1024,128]{1,0:T(8,128)} custom-call(s32[1]{0:T(128)S(6)} %copy.11.refs_0_, f32[1,2,2,128,128]{4,3,2,1,0:T(8,128)} %refs_1_.1, f32[1,2,128,128]{3,2,1,0:T(8,128)} %refs_2_.2, f32[1,1,2,2,128,128]{5,4,3,2,1,0:T(8,128)} %refs_3_.2, f32[1,1,2,2,128,128]{5,4,3,2,1,0:T(8,128)} %refs_4_.1), custom_call_target="tpu_custom_call" | custom-call | tf_op jit(solution)/shard_map/green/pallas_call | solution.py:279
  5.5 0.0 copy-start.1
  5.5 0.0 copy-start.2
  5.5 15.7 %all-to-all-start = ((f32[256,4,128]{2,1,0:T(4,128)}), f32[256,4,128]{2,1,0:T(4,128)S(1)}, u32[]{:S(2)}, u32[]{:S(2)}) async-start(f32[256,4,128]{2,1,0:T(4,128)} %bitcast.9), calls=%async_computation | async-start | bytes 1048576 | tf_op jit(solution)/shard_map/all_to_all | solution.py:296
  21.2 20.4 %all-to-all-done = f32[256,4,128]{2,1,0:T(4,128)S(1)} async-done(((f32[256,4,128]{2,1,0:T(4,128)}), f32[256,4,128]{2,1,0:T(4,128)S(1)}, u32[]{:S(2)}, u32[]{:S(2)}) %all-to-all-start) | async-done | bytes 524320 | tf_op jit(solution)/shard_map/all_to_all | solution.py:296
  41.6 0.0 copy-done.1
  41.6 0.0 copy-done.2
  41.6 2.3 %sigma.1 = (f32[512,128]{1,0:T(8,128)}, bf16[2,512,256]{2,1,0:T(8,128)(2,1)S(1)}, f32[512,256]{1,0:T(8,128)S(1)}, f32[128,128]{1,0:T(8,128)S(1)}) custom-call(s32[1]{0:T(128)S(6)} %select_n.7.refs_0_.refs_1_, f32[1024,128]{1,0:T(8,128)S(1)} %bitcast.7, bf16[2,2,256,128]{3,2,1,0:T(8,128)(2,1)S(1)} %copy-done.2, bf16[2,2,128,256]{3,2,1,0:T(8,128)(2,1)S(1)} %copy-done.1), custom_call_target="tpu_custom_call" | custom-call | tf_op jit(solution)/shard_map/sigma/pallas_call | solution.py:279
  43.9 0.0 copy-start
  43.9 5.9 %all-to-all-start.1 = ((f32[256,2,128]{2,1,0:T(2,128)}), f32[256,2,128]{2,1,0:T(2,128)S(1)}, u32[]{:S(2)}, u32[]{:S(2)}) async-start(f32[256,2,128]{2,1,0:T(2,128)} %bitcast.11), calls=%async_computation.1 | async-start | bytes 524288 | tf_op jit(solution)/shard_map/all_to_all | solution.py:296
  49.9 0.0 copy-done
  49.9 1.2 %polar.1 = (f32[2,128,128]{2,1,0:T(8,128)S(1)}, f32[2,128,128]{2,1,0:T(8,128)S(1)}) custom-call(s32[1]{0:T(128)} %bitcast.6.refs_0_.mom_ref, s32[1]{0:T(128)S(6)} %select_n.7.refs_0_.refs_1_, f32[1024,128]{1,0:T(8,128)S(1)} %bitcast.8, f32[128,128]{1,0:T(8,128)S(1)} %get-tuple-element.9.refs_3_, bf16[2,512,256]{2,1,0:T(8,128)(2,1)S(1)} %get-tuple-element.10.refs_4_, ...), custom_call_target="tpu_custom_call" | custom-call | tf_op jit(solution)/shard_map/polar/pallas_call | solution.py:279
  51.1 1.5 %collective-permute-start = (f32[2,128,128]{2,1,0:T(8,128)S(1)}, f32[2,128,128]{2,1,0:T(8,128)S(1)}, u32[]{:S(2)}, u32[]{:S(2)}) collective-permute-start(f32[2,128,128]{2,1,0:T(8,128)S(1)} %get-tuple-element.13), channel_id=1, source_target_pairs={{0,1},{1,0},{2,3},{3,2},{4,5},{5,4},{6,7},{7,6},{8,9},{9,8},{10,11... | collective-permute-start | bytes 393224 | tf_op jit(solution)/shard_map/ppermute | solution.py:21
  52.6 3.1 %collective-permute-done.other_ref = f32[2,128,128]{2,1,0:T(8,128)S(1)} collective-permute-done((f32[2,128,128]{2,1,0:T(8,128)S(1)}, f32[2,128,128]{2,1,0:T(8,128)S(1)}, u32[]{:S(2)}, u32[]{:S(2)}) %collective-permute-start) | collective-permute-done | bytes 131104 | tf_op jit(solution)/shard_map/ppermute | solution.py:21
  55.7 0.7 %join.1 = f32[1,2,128,256]{3,2,1,0:T(8,128)} custom-call(s32[1]{0:T(128)} %bitcast.6.refs_0_.mom_ref, f32[2,128,128]{2,1,0:T(8,128)S(1)} %get-tuple-element.12.keep_ref, f32[2,128,128]{2,1,0:T(8,128)S(1)} %collective-permute-done.other_ref), custom_call_target="tpu_custom_call" | custom-call | tf_op jit(solution)/shard_map/join/pallas_call | solution.py:279
  56.5 9.0 %all-to-all-done.1 = f32[256,2,128]{2,1,0:T(2,128)S(1)} async-done(((f32[256,2,128]{2,1,0:T(2,128)}), f32[256,2,128]{2,1,0:T(2,128)S(1)}, u32[]{:S(2)}, u32[]{:S(2)}) %all-to-all-start.1) | async-done | bytes 262176 | tf_op jit(solution)/shard_map/all_to_all | solution.py:296
  65.4 0.7 %copy.10 = f32[2,256,128]{2,1,0:T(8,128)} copy(f32[2,256,128]{2,0,1:T(2,128)S(1)} %bitcast.10) | data formatting | bytes 524288 | tf_op jit(solution)/shard_map/transpose | solution.py:362
Async XLA Ops:
  5.5 36.1 %copy-start.1 = (bf16[2,2,128,256]{3,2,1,0:T(8,128)(2,1)S(1)}, bf16[2,2,128,256]{3,2,1,0:T(8,128)(2,1)}, u32[]{:S(2)}) copy-start(bf16[2,2,128,256]{3,2,1,0:T(8,128)(2,1)} %constant.36.clone.refs_3_) | copy-start | bytes 786436
  5.5 36.1 %copy-start.2 = (bf16[2,2,256,128]{3,2,1,0:T(8,128)(2,1)S(1)}, bf16[2,2,256,128]{3,2,1,0:T(8,128)(2,1)}, u32[]{:S(2)}) copy-start(bf16[2,2,256,128]{3,2,1,0:T(8,128)(2,1)} %constant.35.clone.refs_2_) | copy-start | bytes 786436
  5.5 36.1 %all-to-all-start = ((f32[256,4,128]{2,1,0:T(4,128)}), f32[256,4,128]{2,1,0:T(4,128)S(1)}, u32[]{:S(2)}, u32[]{:S(2)}) async-start(f32[256,4,128]{2,1,0:T(4,128)} %bitcast.9), calls=%async_computation | async-start | bytes 1048576 | tf_op jit(solution)/shard_map/all_to_all | solution.py:296
  43.9 5.9 %copy-start = (bf16[2,256,512]{2,1,0:T(8,128)(2,1)S(1)}, bf16[2,256,512]{2,1,0:T(8,128)(2,1)}, u32[]{:S(2)}) copy-start(bf16[2,256,512]{2,1,0:T(8,128)(2,1)} %constant.37.clone.refs_5_) | copy-start | bytes 1572868
  43.9 21.5 %all-to-all-start.1 = ((f32[256,2,128]{2,1,0:T(2,128)}), f32[256,2,128]{2,1,0:T(2,128)S(1)}, u32[]{:S(2)}, u32[]{:S(2)}) async-start(f32[256,2,128]{2,1,0:T(2,128)} %bitcast.11), calls=%async_computation.1 | async-start | bytes 524288 | tf_op jit(solution)/shard_map/all_to_all | solution.py:296
  51.1 4.7 %collective-permute-start = (f32[2,128,128]{2,1,0:T(8,128)S(1)}, f32[2,128,128]{2,1,0:T(8,128)S(1)}, u32[]{:S(2)}, u32[]{:S(2)}) collective-permute-start(f32[2,128,128]{2,1,0:T(8,128)S(1)} %get-tuple-element.13), channel_id=1, source_target_pairs={{0,1},{1,0},{2,3},{3,2},{4,5},{5,4},{6,7},{7,6},{8,9},{9,8},{10,11... | collective-permute-start | bytes 393224 | tf_op jit(solution)/shard_map/ppermute | solution.py:21

commit v5 on v4

--- a/solution.py
+++ b/solution.py
@@ -35,7 +35,9 @@
 
 
 def dot3(left, right):
-    return dot(left[0], right[0]) + (dot(left[0], right[1]) + dot(left[1], right[0]))
+    rows = left[0].shape[0]
+    both = dot(jnp.concatenate(left, axis=0), right[0])
+    return both[:rows] + (dot(left[0], right[1]) + both[rows:])
 
 
 def left_form(pair):
@@ -54,8 +56,11 @@
 
 
 def cproduct(left, right):
-    result = dot3(left, right)
-    order = result.shape[0]
+    order = left[0].shape[0]
+    result = dot(
+        jnp.concatenate([left[0], left[0], left[1]], axis=1),
+        jnp.concatenate([right[0], right[1], right[0]], axis=0),
+    )
     return result[:, :order], result[:, order:]
 
 
@@ -80,7 +85,33 @@
     return 2.0 * first_re - second[0], 2.0 * first_im - second[1]
 
 
-def green_kernel(spacing, map_ref, ham_ref, hop_ref, self_ref, screened_ref, out_ref):
+def green_kernel(
+    spacing,
+    map_ref,
+    ham_hbm,
+    hop_hbm,
+    self_hbm,
+    screened_hbm,
+    out_ref,
+    ham_ref,
+    hop_ref,
+    self_ref,
+    screened_ref,
+    semaphores,
+):
+    copies = [
+        pltpu.make_async_copy(source, target, semaphores.at[n])
+        for n, (source, target) in enumerate(
+            (
+                (ham_hbm, ham_ref),
+                (self_hbm, self_ref),
+                (hop_hbm, hop_ref),
+                (screened_hbm, screened_ref),
+            )
+        )
+    ]
+    for copy in copies:
+        copy.start()
     order = ham_ref.shape[3]
     rows = lax.broadcasted_iota(jnp.int32, (order, order), 0)
     cols = lax.broadcasted_iota(jnp.int32, (order, order), 1)
@@ -101,17 +132,21 @@
             jnp.where(eye, broadening, 0.0) - herm_im - self_ref[0, 0, 1, block],
         )
 
+    copies[0].wait()
+    copies[1].wait()
+    local = approx_inverse(*shifted(0), eye)
+    last = shifted(1)
+    copies[2].wait()
+    copies[3].wait()
     for block in range(2):
         put(block, 2, screened_ref[0, 0, 0, block])
         put(block, 3, screened_ref[0, 0, 1, block])
     hop = (hop_ref[0, 0], hop_ref[0, 1])
     adjoint = (hop[0].T, -hop[1].T)
     hop_right = right_form(hop)
-    local = approx_inverse(*shifted(0), eye)
     incoming = cproduct(left_form(adjoint), right_form(local))
     outgoing = cproduct(left_form(local), hop_right)
     coupled = cproduct(left_form(incoming), hop_right)
-    last = shifted(1)
     green = approx_inverse(last[0] - coupled[0], last[1] - coupled[1], eye)
     middle = cproduct(left_form(outgoing), right_form(green))
     middle = cproduct(left_form(middle), right_form(incoming))
@@ -271,15 +306,17 @@
     out_ref[0, :, :, order:] = jnp.where(first, other_ref[...], keep_ref[...])
 
 
-def call(kernel, outs, scalars, name, scratch=()):
+def call(kernel, outs, scalars, name, scratch=(), hbm=False):
     vmem = pl.BlockSpec(memory_space=pltpu.VMEM)
     smem = pl.BlockSpec(memory_space=pltpu.SMEM)
+
+    source = pl.BlockSpec(memory_space=pltpu.HBM) if hbm else vmem
 
     def run(*operands):
         return pl.pallas_call(
             kernel,
             out_shape=outs,
-            in_specs=[smem] * scalars + [vmem] * (len(operands) - scalars),
+            in_specs=[smem] * scalars + [source] * (len(operands) - scalars),
             out_specs=jax.tree.map(lambda _: vmem, outs),
             scratch_shapes=list(scratch),
             name=name,
@@ -324,9 +361,13 @@
 
     targets = 2 * slots
     column = lax.axis_index(("energy", "mom")).astype(jnp.int32).reshape(1) % order
+    sources = (hamiltonian, hopping, self_energy, screened)
     fields = call(
-        lambda *refs: green_kernel(spacing, *refs), f32(targets * field_rows, order), 1, "green"
-    )(energy_map, hamiltonian, hopping, self_energy, screened)
+        lambda *refs: green_kernel(spacing, *refs), f32(targets * field_rows, order), 1, "green",
+        [pltpu.VMEM(array.shape, jnp.float32) for array in sources]
+        + [pltpu.SemaphoreType.DMA((4,))],
+        hbm=True,
+    )(energy_map, *sources)
     own = resident(exchange(fields.reshape(targets, field_rows, order)).reshape(fields.shape))
     send, forward, lesser_hat, occupied = call(
         lambda *refs: sigma_kernel(spacing, *refs),

time: 66.4 us -> 66.3 us (level)
  no operation moved by 1% of the time
where the time goes in v5:
time: 66.3 us; the launch traced here: 66.1 us
  waiting for transfers between devices  32.6 us (49%)
  starting transfers between devices  23.1 us (35%)
  Pallas kernels  8.31 us (13%)
  between operations  1.35 us (2%)
  local copies, waits for them, and re-layouts  0.74 us (1%)
    all_to_all x2, waiting for transfers between devices, exchange(): lax.all_to_all(chunks, ('energy', 'mom'), split_axis=0, concat_axis=0, ti...  29.4 us
    all_to_all x2, starting transfers between devices, exchange(): lax.all_to_all(chunks, ('energy', 'mom'), split_axis=0, concat_axis=0, ti...  21.6 us
    pallas_call x4, Pallas kernels, run(): pl.pallas_call(kernel, out_shape=outs, in_specs=[smem] * scalars + [sourc...  8.31 us
    ppermute x1, waiting for transfers between devices, from_partner(): lax.ppermute(array, axis, [(i, i ^ 1) for i in range(lax.axis_size(axis))])  3.15 us
    ppermute x1, starting transfers between devices, from_partner(): lax.ppermute(array, axis, [(i, i ^ 1) for i in range(lax.axis_size(axis))])  1.53 us
  transfers between devices with their start and end apart: 3, of which 3 were waited for; matrix products, arithmetic and copies ran while one was open for 0% of the time, Pallas kernels for 3%

profile of v5, /device:TPU:1, one launch (start us, length us, event | category | flops | bytes accessed | tf_op | source)
XLA Modules:
  0.0 66.1 jit_solution(11905483221745635217)
XLA Ops:
  1.3 4.1 %green.1 = f32[1024,128]{1,0:T(8,128)} custom-call(s32[1]{0:T(128)S(6)} %copy.11.refs_0_, f32[1,2,2,128,128]{4,3,2,1,0:T(8,128)} %refs_1_.1, f32[1,2,128,128]{3,2,1,0:T(8,128)} %refs_2_.2, f32[1,1,2,2,128,128]{5,4,3,2,1,0:T(8,128)} %refs_3_.2, f32[1,1,2,2,128,128]{5,4,3,2,1,0:T(8,128)} %refs_4_.1), custom_call_target="tpu_custom_call" | custom-call | tf_op jit(solution)/shard_map/green/pallas_call | solution.py:316
  5.4 0.0 copy-start.1
  5.4 0.0 copy-start.2
  5.4 15.7 %all-to-all-start = ((f32[256,4,128]{2,1,0:T(4,128)}), f32[256,4,128]{2,1,0:T(4,128)S(1)}, u32[]{:S(2)}, u32[]{:S(2)}) async-start(f32[256,4,128]{2,1,0:T(4,128)} %bitcast.9), calls=%async_computation | async-start | bytes 1048576 | tf_op jit(solution)/shard_map/all_to_all | solution.py:333
  21.1 20.4 %all-to-all-done = f32[256,4,128]{2,1,0:T(4,128)S(1)} async-done(((f32[256,4,128]{2,1,0:T(4,128)}), f32[256,4,128]{2,1,0:T(4,128)S(1)}, u32[]{:S(2)}, u32[]{:S(2)}) %all-to-all-start) | async-done | bytes 524320 | tf_op jit(solution)/shard_map/all_to_all | solution.py:333
  41.6 0.0 copy-done.1
  41.6 0.0 copy-done.2
  41.6 2.3 %sigma.1 = (f32[512,128]{1,0:T(8,128)}, bf16[2,512,256]{2,1,0:T(8,128)(2,1)S(1)}, f32[512,256]{1,0:T(8,128)S(1)}, f32[128,128]{1,0:T(8,128)S(1)}) custom-call(s32[1]{0:T(128)S(6)} %select_n.7.refs_0_.refs_1_, f32[1024,128]{1,0:T(8,128)S(1)} %bitcast.7, bf16[2,2,256,128]{3,2,1,0:T(8,128)(2,1)S(1)} %copy-done.2, bf16[2,2,128,256]{3,2,1,0:T(8,128)(2,1)S(1)} %copy-done.1), custom_call_target="tpu_custom_call" | custom-call | tf_op jit(solution)/shard_map/sigma/pallas_call | solution.py:316
  43.9 0.0 copy-start
  43.9 5.9 %all-to-all-start.1 = ((f32[256,2,128]{2,1,0:T(2,128)}), f32[256,2,128]{2,1,0:T(2,128)S(1)}, u32[]{:S(2)}, u32[]{:S(2)}) async-start(f32[256,2,128]{2,1,0:T(2,128)} %bitcast.11), calls=%async_computation.1 | async-start | bytes 524288 | tf_op jit(solution)/shard_map/all_to_all | solution.py:333
  49.8 0.0 copy-done
  49.8 1.2 %polar.1 = (f32[2,128,128]{2,1,0:T(8,128)S(1)}, f32[2,128,128]{2,1,0:T(8,128)S(1)}) custom-call(s32[1]{0:T(128)} %bitcast.6.refs_0_.mom_ref, s32[1]{0:T(128)S(6)} %select_n.7.refs_0_.refs_1_, f32[1024,128]{1,0:T(8,128)S(1)} %bitcast.8, f32[128,128]{1,0:T(8,128)S(1)} %get-tuple-element.9.refs_3_, bf16[2,512,256]{2,1,0:T(8,128)(2,1)S(1)} %get-tuple-element.10.refs_4_, ...), custom_call_target="tpu_custom_call" | custom-call | tf_op jit(solution)/shard_map/polar/pallas_call | solution.py:316
  51.0 1.5 %collective-permute-start = (f32[2,128,128]{2,1,0:T(8,128)S(1)}, f32[2,128,128]{2,1,0:T(8,128)S(1)}, u32[]{:S(2)}, u32[]{:S(2)}) collective-permute-start(f32[2,128,128]{2,1,0:T(8,128)S(1)} %get-tuple-element.13), channel_id=1, source_target_pairs={{0,1},{1,0},{2,3},{3,2},{4,5},{5,4},{6,7},{7,6},{8,9},{9,8},{10,11... | collective-permute-start | bytes 393224 | tf_op jit(solution)/shard_map/ppermute | solution.py:21
  52.5 3.1 %collective-permute-done.other_ref = f32[2,128,128]{2,1,0:T(8,128)S(1)} collective-permute-done((f32[2,128,128]{2,1,0:T(8,128)S(1)}, f32[2,128,128]{2,1,0:T(8,128)S(1)}, u32[]{:S(2)}, u32[]{:S(2)}) %collective-permute-start) | collective-permute-done | bytes 131104 | tf_op jit(solution)/shard_map/ppermute | solution.py:21
  55.7 0.7 %join.1 = f32[1,2,128,256]{3,2,1,0:T(8,128)} custom-call(s32[1]{0:T(128)} %bitcast.6.refs_0_.mom_ref, f32[2,128,128]{2,1,0:T(8,128)S(1)} %get-tuple-element.12.keep_ref, f32[2,128,128]{2,1,0:T(8,128)S(1)} %collective-permute-done.other_ref), custom_call_target="tpu_custom_call" | custom-call | tf_op jit(solution)/shard_map/join/pallas_call | solution.py:316
  56.4 9.0 %all-to-all-done.1 = f32[256,2,128]{2,1,0:T(2,128)S(1)} async-done(((f32[256,2,128]{2,1,0:T(2,128)}), f32[256,2,128]{2,1,0:T(2,128)S(1)}, u32[]{:S(2)}, u32[]{:S(2)}) %all-to-all-start.1) | async-done | bytes 262176 | tf_op jit(solution)/shard_map/all_to_all | solution.py:333
  65.4 0.7 %copy.10 = f32[2,256,128]{2,1,0:T(8,128)} copy(f32[2,256,128]{2,0,1:T(2,128)S(1)} %bitcast.10) | data formatting | bytes 524288 | tf_op jit(solution)/shard_map/transpose | solution.py:403
Async XLA Ops:
  5.4 36.2 %copy-start.1 = (bf16[2,2,128,256]{3,2,1,0:T(8,128)(2,1)S(1)}, bf16[2,2,128,256]{3,2,1,0:T(8,128)(2,1)}, u32[]{:S(2)}) copy-start(bf16[2,2,128,256]{3,2,1,0:T(8,128)(2,1)} %constant.36.clone.refs_3_) | copy-start | bytes 786436
  5.4 36.1 %copy-start.2 = (bf16[2,2,256,128]{3,2,1,0:T(8,128)(2,1)S(1)}, bf16[2,2,256,128]{3,2,1,0:T(8,128)(2,1)}, u32[]{:S(2)}) copy-start(bf16[2,2,256,128]{3,2,1,0:T(8,128)(2,1)} %constant.35.clone.refs_2_) | copy-start | bytes 786436
  5.4 36.1 %all-to-all-start = ((f32[256,4,128]{2,1,0:T(4,128)}), f32[256,4,128]{2,1,0:T(4,128)S(1)}, u32[]{:S(2)}, u32[]{:S(2)}) async-start(f32[256,4,128]{2,1,0:T(4,128)} %bitcast.9), calls=%async_computation | async-start | bytes 1048576 | tf_op jit(solution)/shard_map/all_to_all | solution.py:333
  43.9 5.9 %copy-start = (bf16[2,256,512]{2,1,0:T(8,128)(2,1)S(1)}, bf16[2,256,512]{2,1,0:T(8,128)(2,1)}, u32[]{:S(2)}) copy-start(bf16[2,256,512]{2,1,0:T(8,128)(2,1)} %constant.37.clone.refs_5_) | copy-start | bytes 1572868
  43.9 21.5 %all-to-all-start.1 = ((f32[256,2,128]{2,1,0:T(2,128)}), f32[256,2,128]{2,1,0:T(2,128)S(1)}, u32[]{:S(2)}, u32[]{:S(2)}) async-start(f32[256,2,128]{2,1,0:T(2,128)} %bitcast.11), calls=%async_computation.1 | async-start | bytes 524288 | tf_op jit(solution)/shard_map/all_to_all | solution.py:333
  51.0 4.7 %collective-permute-start = (f32[2,128,128]{2,1,0:T(8,128)S(1)}, f32[2,128,128]{2,1,0:T(8,128)S(1)}, u32[]{:S(2)}, u32[]{:S(2)}) collective-permute-start(f32[2,128,128]{2,1,0:T(8,128)S(1)} %get-tuple-element.13), channel_id=1, source_target_pairs={{0,1},{1,0},{2,3},{3,2},{4,5},{5,4},{6,7},{7,6},{8,9},{9,8},{10,11... | collective-permute-start | bytes 393224 | tf_op jit(solution)/shard_map/ppermute | solution.py:21
